TPU v7x, 32 devices: a whole 2x2x4 slice. The times are simulated.
32 devices in a mesh: tri: 4 (over z), colx: 4 (over x, core), coly: 2 (over y).
Axes of the slice: x: 2, y: 2, z: 4, core: 2. Of those that a mesh axis runs over, the one named last changes fastest.
Arguments:
- weight: float32 [13824, 5120], P(('colx', 'coly'), 'tri'), may hold values from -6 to 6
- tiles: int32 [48, 3], replicated, may hold values from 0 to 19, as said below
Outputs:
- correction: float32 [13824, 5120], P(('colx', 'coly'), 'tri')
- updated: float32 [13824, 5120], P(('colx', 'coly'), 'tri')
Inputs may be any that keep to these rules, and one draw needn't show every extreme that they name: `tiles`: each row is (i, j, owner) with i <= j < 20 and owner < 4; no pair is listed twice; one owner has exactly 24 rows and every other owner at most 24; the rows stand in no particular order.
All inputs are finite; a program needn't handle non-finite values.
Results may differ from a plain program's by a relative error of at most 0.0003.
Values sent between devices are 32-bit elements; how exact they have to be, the bound alone decides.
No kernel may reach another device: no remote copies, remote signals or barrier semaphores. Data moves between devices by JAX's collectives and lax.ppermute only.
A program may use at most 192 MiB of HBM per device.

v0:
```python
import jax
import jax.numpy as jnp
from jax import lax
from jax.sharding import PartitionSpec as P

ROWS = 5120
COLS = 13824
PANEL = 256
PANEL_COUNT = 20
TILES = 48


def on_device(weight, tiles):
    top_precision = lax.Precision.HIGHEST
    whole = lax.all_gather(weight, "tri", axis=1, tiled=True)
    local_cols = whole.shape[0]
    panels = whole.reshape(local_cols, PANEL_COUNT, PANEL)
    my_index = lax.axis_index("tri")
    owners = lax.axis_size("tri")
    pair_slot_count = TILES // owners
    share = lax.dynamic_slice_in_dim(tiles, my_index * pair_slot_count, pair_slot_count, 0)
    left_index = share[:, 0]
    right_index = share[:, 1]
    valid = jnp.ones((pair_slot_count,), jnp.float32)
    left = jnp.take(panels, left_index, axis=1)
    right = jnp.take(panels, right_index, axis=1)
    partial_gram = jnp.einsum(
        "cka,ckb->kab", left, right, precision=top_precision, preferred_element_type=jnp.float32
    )
    partial_gram = partial_gram * valid[:, None, None]
    gram = lax.psum(partial_gram, ("colx", "coly")) / COLS
    upper_panel = jnp.einsum(
        "kab,ckb->cka", gram, right, precision=top_precision, preferred_element_type=jnp.float32
    )
    lower_panel = jnp.einsum(
        "kab,cka->ckb", gram, left, precision=top_precision, preferred_element_type=jnp.float32
    )
    off_diag = (left_index != right_index).astype(jnp.float32)
    lower_panel = lower_panel * off_diag[None, :, None]
    panel_ids = jnp.arange(PANEL_COUNT, dtype=jnp.int32)
    leftward_send = (panel_ids[:, None] == left_index[None, :]).astype(jnp.float32)
    rightward_send = (panel_ids[:, None] == right_index[None, :]).astype(jnp.float32)
    total = jnp.einsum(
        "tl,hlx->htx",
        leftward_send,
        upper_panel,
        precision=top_precision,
        preferred_element_type=jnp.float32,
    )
    total = total + jnp.einsum(
        "tl,hlx->htx",
        rightward_send,
        lower_panel,
        precision=top_precision,
        preferred_element_type=jnp.float32,
    )
    correction = lax.psum_scatter(
        total.reshape(local_cols, ROWS), "tri", scatter_dimension=1, tiled=True
    )
    updated = 1.5 * weight - 0.5 * correction
    return (correction, updated)


def solution(mesh):
    in_specs = (P(("colx", "coly"), "tri"), P())
    out_specs = (P(("colx", "coly"), "tri"), P(("colx", "coly"), "tri"))
    return jax.shard_map(
        on_device, mesh=mesh, in_specs=in_specs, out_specs=out_specs, check_vma=False
    )
```

profile of v0, /device:TPU:0, one launch (start us, length us, event | category | flops | bytes accessed | tf_op | source)
XLA Modules:
  0.0 1653.7 jit_solution(13465962570519255034)
XLA Ops:
  7.2 0.0 copy-start
  7.2 0.0 all-gather.2.cloned.1.call-start
  7.2 0.7 all-gather.2.cloned.1.call-update
  7.9 0.0 all-reduce.2.cloned.1.call-start
  8.0 0.0 copy-done
  8.0 0.1 constant_dynamic-slice_fusion
  8.0 0.5 compare_and_fusion
  8.6 596.6 %all-gather.2.cloned.1.call-done = f32[1728,5120]{1,0:T(8,128)} async-done(((f32[1728,1280]{1,0:T(8,128)}), f32[1728,5120]{1,0:T(8,128)}) %all-gather.2.cloned.1.call-update) | async-done | bytes 35389456 | tf_op jit(solution)/shard_map/all_gather | solution.py:15
  605.2 34.0 %copy.4 = f32[1728,5120]{0,1:T(8,128)} copy(f32[1728,5120]{1,0:T(8,128)} %all-gather.2.cloned.1.call-done) | data formatting | bytes 70778880 | tf_op jit(solution)/shard_map/all_gather | solution.py:15
  639.2 34.4 %copy.5 = f32[1728,20,256]{2,0,1:T(8,128)} copy(f32[1728,20,256]{0,2,1:T(8,128)} %bitcast.43) | data formatting | bytes 70778880 | tf_op jit(solution)/shard_map/reshape | solution.py:17
  673.6 17.6 %gather_fusion.1 = f32[12,1728,256]{2,1,0:T(8,128)} fusion(f32[1728,20,256]{2,0,1:T(8,128)} %copy.5, s32[1024]{0:T(1024)S(1)} %get-tuple-element.14), kind=kCustom, calls=%fused_computation.1.clone | custom fusion | bytes 42467376 | tf_op jit(solution)/shard_map/jit(_take)/gather | solution.py:25
  691.2 16.4 gather_fusion
  707.6 43.0 %fusion.7 = f32[12,256,256]{2,1,0:T(8,128)} fusion(f32[12,1728,256]{2,1,0:T(8,128)} %gather_fusion.1, f32[12,1728,256]{2,1,0:T(8,128)} %gather_fusion, pred[12]{0:T(512)(128)(4,1)S(1)} %get-tuple-element.5, pred[12]{0:T(512)(128)(4,1)S(1)} %get-tuple-element.12), kind=kOutput, calls=%fused_computation.11 | convolution fusion | flops 16318070784 | bytes 45613080 | tf_op jit(solution)/shard_map/cka,ckb->kab/dot_general | solution.py:27
  750.6 0.0 all-reduce.2.cloned.1.call-update
  750.7 0.0 reduce-scatter.2.cloned.1.call-start
  750.7 70.1 %all-reduce.2.cloned.1.call-done = f32[12,256,256]{2,1,0:T(8,128)} async-done(((f32[12,256,256]{2,1,0:T(8,128)}), f32[12,256,256]{2,1,0:T(8,128)}) %all-reduce.2.cloned.1.call-update) | async-done | bytes 3145744 | tf_op jit(solution)/shard_map/psum | solution.py:31
  820.8 26.9 %fusion.9 = f32[12,1728,256]{2,1,0:T(8,128)} fusion(f32[12,1728,256]{2,1,0:T(8,128)} %gather_fusion, pred[12]{0:T(512)(128)(4,1)S(1)} %get-tuple-element.12, f32[12,256,256]{2,1,0:T(8,128)} %all-reduce.2.cloned.1.call-done), kind=kOutput, calls=%fused_computation.13 | convolution fusion | flops 16313548800 | bytes 45613068 | tf_op jit(solution)/shard_map/kab,ckb->cka/dot_general | solution.py:32
  847.7 0.0 copy-start.2
  847.7 50.8 %fusion.2 = f32[1728,256,20]{1,2,0:T(8,128)} fusion(f32[12,1728,256]{2,1,0:T(8,128)} %fusion.9, s32[12]{0:T(128)S(1)} %get-tuple-element.10), kind=kOutput, calls=%fused_computation.5 | convolution fusion | flops 1274020096 | bytes 56623152 | tf_op jit(solution)/shard_map/tl,hlx->htx/dot_general | solution.py:43
  898.5 0.0 copy-done.2
  898.5 0.0 copy-start.3
  898.5 25.0 %fusion.5 = f32[12,1728,256]{2,1,0:T(8,128)} fusion(f32[12,1728,256]{2,1,0:T(8,128)} %gather_fusion.1, pred[12]{0:T(512)(128)(4,1)S(1)} %get-tuple-element.5, f32[12,256,256]{2,1,0:T(8,128)S(1)} %copy-done.2), kind=kOutput, calls=%fused_computation.9 | convolution fusion | flops 16313548800 | bytes 45613068 | tf_op jit(solution)/shard_map/kab,cka->ckb/dot_general | solution.py:35
  923.5 0.0 copy-done.3
  923.5 48.5 %add_bitcast_fusion = f32[1728,20,256]{2,1,0:T(8,128)} fusion(f32[1728,256,20]{1,2,0:T(8,128)} %fusion.2, f32[12,1728,256]{2,1,0:T(8,128)} %fusion.5, f32[12]{0:T(128)S(1)} %copy-done.3, s32[12]{0:T(128)S(1)} %get-tuple-element.9), kind=kOutput, calls=%fused_computation.2 | convolution fusion | flops 1288175872 | bytes 92012640 | tf_op jit(solution)/shard_map/tl,hlx->htx/dot_general | solution.py:50
  972.0 39.6 %copy.7 = f32[1728,20,256]{0,2,1:T(8,128)} copy(f32[1728,20,256]{2,1,0:T(8,128)} %add_bitcast_fusion) | data formatting | bytes 70778880 | tf_op jit(solution)/shard_map/add | solution.py:50
  1011.6 0.0 reduce-scatter.2.cloned.1.call-update
  1011.6 10.4 copy.8
  1022.1 592.3 %reduce-scatter.2.cloned.1.call-done = f32[1728,1280]{0,1:T(8,128)} async-done(((f32[1728,5120]{0,1:T(8,128)}), f32[1728,1280]{0,1:T(8,128)}) %reduce-scatter.2.cloned.1.call-update) | async-done | bytes 8847376 | tf_op jit(solution)/shard_map/reduce_scatter | solution.py:57
  1614.4 0.0 copy-start.1
  1614.4 10.9 multiply_subtract_fusion
  1625.3 10.7 copy.10
  1636.0 10.7 copy.9
  1646.7 0.0 copy-done.1
  (2 shorter events, 0.0 us)
Async XLA Ops:
  7.2 0.8 copy-start
  7.2 598.0 %all-gather.2.cloned.1.call-start = ((), (), s32[]{:S(2)}) async-start(), calls=%async_computation.1 | async-start | bytes 44236800 | tf_op jit(solution)/shard_map/all_gather | solution.py:15
  7.9 812.9 %all-reduce.2.cloned.1.call-start = ((), (), s32[]{:S(2)}) async-start(), calls=%async_computation.2 | async-start | bytes 6291456 | tf_op jit(solution)/shard_map/psum | solution.py:31
  750.7 863.7 %reduce-scatter.2.cloned.1.call-start = ((), (), s32[]{:S(2)}) async-start(), calls=%async_computation.3 | async-start | bytes 45875200 | tf_op jit(solution)/shard_map/reduce_scatter | solution.py:57
  847.7 50.8 %copy-start.2 = (f32[12,256,256]{2,1,0:T(8,128)S(1)}, f32[12,256,256]{2,1,0:T(8,128)}, u32[]{:S(2)}) copy-start(f32[12,256,256]{2,1,0:T(8,128)} %all-reduce.2.cloned.1.call-done) | copy-start | bytes 9437188
  898.5 25.0 %copy-start.3 = (f32[12]{0:T(128)S(1)}, f32[12]{0:T(128)}, u32[]{:S(2)}) copy-start(f32[12]{0:T(128)} %get-tuple-element.11) | copy-start | bytes 148
  1614.4 32.3 %copy-start.1 = (s32[48,3]{0,1:T(4,128)S(1)}, s32[48,3]{0,1:T(4,128)}, u32[]{:S(2)}) copy-start(s32[48,3]{0,1:T(4,128)} %param.5) | copy-start | bytes 1732
Sparse Core Ops, SparseCore 0:
  9.6 595.6 all-gather.1
  750.8 69.9 all-reduce.1
  1011.8 602.5 reduce-scatter.1
where the time goes:
time: 1660 us; the launch traced here: 1650 us
  waiting for transfers between devices  1260 us (76%)
  matrix products  194 us (12%)
  local copies, waits for them, and re-layouts  174 us (10%)
    all_gather x1, waiting for transfers between devices, on_device(): whole = lax.all_gather(weight, 'tri', axis=1, tiled=True)  597 us
    reduce_scatter x1, waiting for transfers between devices, on_device(): lax.psum_scatter(total.reshape(local_cols, ROWS), 'tri', scatter_dimensio...  592 us
    psum x1, waiting for transfers between devices, on_device(): gram = lax.psum(partial_gram, ('colx', 'coly')) / COLS  70.1 us
    dot_general x1, matrix products, on_device(): jnp.einsum('tl,hlx->htx', leftward_send, upper_panel, precision=top_preci...  50.8 us
    dot_general x1, matrix products, on_device(): jnp.einsum('tl,hlx->htx', rightward_send, lower_panel, precision=top_prec...  48.5 us
    dot_general x1, matrix products, on_device(): jnp.einsum('cka,ckb->kab', left, right, precision=top_precision, preferre...  43 us
    add x1, local copies, waits for them, and re-layouts, on_device(): total + jnp.einsum('tl,hlx->htx', rightward_send, lower_panel, precision=...  39.6 us
    reshape x1, local copies, waits for them, and re-layouts, on_device(): panels = whole.reshape(local_cols, PANEL_COUNT, PANEL)  34.4 us
  transfers between devices with their start and end apart: 3, of which 3 were waited for; matrix products, arithmetic and copies ran while one was open for 1% of the time, Pallas kernels for 0%

commit v1 on v0

v1 whole, which is shorter than its diff:
```python
import functools

import jax
import jax.numpy as jnp
from jax import lax
from jax.experimental import pallas as pl
from jax.experimental.pallas import tpu as pltpu
from jax.sharding import PartitionSpec as P

PANEL = 256
VMEM_LIMIT = 56 * 1024 * 1024
GROUP = 4


def split(x):
    high = x.astype(jnp.bfloat16)
    low = (x - high.astype(jnp.float32)).astype(jnp.bfloat16)
    return high, low


def product(left, right, dims):
    (lh, ll), (rh, rl) = left, right

    def dot(a, b):
        return lax.dot_general(a, b, (dims, ((), ())), preferred_element_type=jnp.float32)

    return dot(lh, rh) + (dot(lh, rl) + dot(ll, rh))


def gram_kernel(scale, n, per, where, *refs):
    pieces = refs[:n]
    gram, high, low, turned_high, turned_low = refs[n:]
    step = pl.program_id(0)

    @pl.when(step == 0)
    def _():
        for d in range(n):
            for s in range(per):
                x = pieces[d][:, s * PANEL : (s + 1) * PANEL]
                h, l = split(x)
                high[d * per + s] = h
                low[d * per + s] = l
                h, l = split(x.T)
                turned_high[d * per + s] = h
                turned_low[d * per + s] = l

    for t in range(GROUP):
        k = step * GROUP + t
        i, j = where[k, 0], where[k, 1]
        gram[t] = scale * product(
            (turned_high[i], turned_low[i]), (high[j], low[j]), ((1,), (0,))
        )


def gram_call(where, pieces, scale):
    n = len(pieces)
    rows, width = pieces[0].shape
    per = width // PANEL
    count = where.shape[0]
    whole = pl.BlockSpec((rows, width), lambda k, w: (0, 0), pipeline_mode=pl.Buffered(1))
    kept = pl.BlockSpec((n * per, rows, PANEL), lambda k, w: (0, 0, 0), pipeline_mode=pl.Buffered(1))
    return pl.pallas_call(
        functools.partial(gram_kernel, scale, n, per),
        grid_spec=pltpu.PrefetchScalarGridSpec(
            num_scalar_prefetch=1,
            grid=(count // GROUP,),
            in_specs=[whole] * n,
            out_specs=[pl.BlockSpec((GROUP, PANEL, PANEL), lambda k, w: (k, 0, 0)), kept, kept],
            scratch_shapes=[pltpu.VMEM((n * per, PANEL, rows), jnp.bfloat16)] * 2,
        ),
        out_shape=[
            jax.ShapeDtypeStruct((count, PANEL, PANEL), jnp.float32),
            jax.ShapeDtypeStruct((n * per, rows, PANEL), jnp.bfloat16),
            jax.ShapeDtypeStruct((n * per, rows, PANEL), jnp.bfloat16),
        ],
        compiler_params=pltpu.CompilerParams(
            dimension_semantics=("arbitrary",), vmem_limit_bytes=VMEM_LIMIT
        ),
        cost_estimate=pl.CostEstimate(
            flops=6 * count * PANEL * PANEL * rows,
            bytes_accessed=8 * n * rows * width + 4 * count * PANEL * PANEL,
            transcendentals=0,
        ),
        name="gram",
    )(where, *pieces)


BLOCK = 8


def correction_kernel(table, gram, high, low, out):
    step = pl.program_id(0)

    @pl.when(step == 0)
    def _():
        out[...] = jnp.zeros_like(out)

    def one(t, carry):
        k = step * BLOCK + t
        i, j, first, second = table[k, 0], table[k, 1], table[k, 2], table[k, 3]

        @pl.when(first >= 0)
        def _():
            at = pl.ds(pl.multiple_of(first * PANEL, PANEL), PANEL)
            out[:, at] += product((high[j], low[j]), split(gram[t]), ((1,), (1,)))

        @pl.when(second >= 0)
        def _():
            at = pl.ds(pl.multiple_of(second * PANEL, PANEL), PANEL)
            out[:, at] += product((high[i], low[i]), split(gram[t]), ((1,), (0,)))

        return carry

    lax.fori_loop(0, BLOCK, one, 0)


def correction_call(table, gram, high, low, per):
    slots, rows, _ = high.shape
    count = table.shape[0]
    kept = pl.BlockSpec((slots, rows, PANEL), lambda k, w: (0, 0, 0), pipeline_mode=pl.Buffered(1))
    return pl.pallas_call(
        correction_kernel,
        grid_spec=pltpu.PrefetchScalarGridSpec(
            num_scalar_prefetch=1,
            grid=(count // BLOCK,),
            in_specs=[pl.BlockSpec((BLOCK, PANEL, PANEL), lambda k, w: (k, 0, 0)), kept, kept],
            out_specs=pl.BlockSpec((rows, per * PANEL), lambda k, w: (0, 0), pipeline_mode=pl.Buffered(1)),
        ),
        out_shape=jax.ShapeDtypeStruct((rows, per * PANEL), jnp.float32),
        compiler_params=pltpu.CompilerParams(
            dimension_semantics=("arbitrary",), vmem_limit_bytes=VMEM_LIMIT
        ),
        cost_estimate=pl.CostEstimate(
            flops=3 * count * PANEL * PANEL * rows,
            bytes_accessed=4 * slots * rows * PANEL + 4 * count * PANEL * PANEL,
            transcendentals=0,
        ),
        name="correction",
    )(table, gram, high, low)


def on_device(columns, weight, tiles):
    n = lax.axis_size("tri")
    z = lax.axis_index("tri")
    local, width = weight.shape
    per = width // PANEL
    rows = -(-local // (n * 16)) * 16
    padded = jnp.pad(weight, ((0, n * rows - local), (0, 0))) if n * rows != local else weight

    def ring(d):
        return [(s, (s + d) % n) for s in range(n)]

    def chunk(d):
        return lax.dynamic_slice_in_dim(padded, lax.rem(z + d, n) * rows, rows, 0)

    pieces = [None] * n
    order = sorted(range(1, n), key=lambda d: abs(d - n // 2))
    for d in order:
        pieces[d] = lax.ppermute(chunk(d), "tri", ring(d))
    pieces[0] = chunk(0)

    first, second = tiles[:, 0], tiles[:, 1]

    def place(panel):
        return lax.rem(z - panel // per + n, n) * per + panel % per

    where = jnp.stack([place(first), place(second)], axis=1)
    gram, high, low = gram_call(where, pieces, 1.0 / columns)
    gram = lax.psum(gram, ("tri", "colx", "coly"))

    def target(panel, d):
        return jnp.where(panel // per == lax.rem(z + d, n), panel % per, -1)

    results = [None] * n
    for d in order + [0]:
        onto = jnp.where(first == second, -1, target(second, d))
        table = jnp.stack([place(first), place(second), target(first, d), onto], axis=1)
        part = correction_call(table, gram, high, low, per)
        results[d] = lax.ppermute(part, "tri", ring(d)) if d else part

    correction = jnp.zeros_like(padded)
    updated = padded
    for d in [0] + order:
        at = lax.rem(z - d + n, n) * rows
        old = lax.dynamic_slice_in_dim(padded, at, rows, 0)
        correction = lax.dynamic_update_slice_in_dim(correction, results[d], at, 0)
        updated = lax.dynamic_update_slice_in_dim(updated, 1.5 * old - 0.5 * results[d], at, 0)
    return correction[:local], updated[:local]


def solution(mesh):
    spec = P(("colx", "coly"), "tri")

    def step(weight, tiles):
        body = jax.shard_map(
            functools.partial(on_device, weight.shape[0]),
            mesh=mesh,
            in_specs=(spec, P()),
            out_specs=(spec, spec),
            check_vma=False,
        )
        return body(weight, tiles)

    return step
```

time: 1660 us -> 685 us (0.41)
  waiting for transfers between devices: 1260 us -> 531 us
  matrix products: 194 us -> 0 us
  local copies, waits for them, and re-layouts: 174 us -> 21.8 us
  Pallas kernels: 0 us -> 89.7 us
    all_gather x1 -> x0, waiting for transfers between devices: 597 us -> none  [on_device(): whole = lax.all_gather(weight, 'tri', axis=1, tiled=True)]
    reduce_scatter x1 -> x0, waiting for transfers between devices: 592 us -> none  [on_device(): lax.psum_scatter(total.reshape(local_cols, ROWS), 'tri', scatter_dimensio...]
    ppermute x0 -> x6, waiting for transfers between devices: none -> 254 us  [the longest x3 141 us: on_device(): pieces[d] = lax.ppermute(chunk(d), 'tri', ring(d))]
    psum x1, waiting for transfers between devices: 70.1 us -> 276 us  [on_device(): gram = lax.psum(gram, ('tri', 'colx', 'coly'))]
    dot_general x5 -> x0, matrix products: 194 us -> none  [the longest x1 50.8 us: on_device(): jnp.einsum('tl,hlx->htx', leftward_send, upper_panel, precision=top_preci...]
    pallas_call x0 -> x5, Pallas kernels: none -> 89.7 us  [the longest x4 66.8 us: correction_call(): pl.pallas_call(correction_kernel, grid_spec=pltpu.PrefetchScalarGridSpec(...]
    add x1 -> x0, local copies, waits for them, and re-layouts: 39.6 us -> none  [on_device(): total + jnp.einsum('tl,hlx->htx', rightward_send, lower_panel, precision=...]
    reshape x1 -> x0, local copies, waits for them, and re-layouts: 34.4 us -> none  [on_device(): panels = whole.reshape(local_cols, PANEL_COUNT, PANEL)]
  transfers between devices with their start and end apart: 3 -> 7, of which waited for: 3 -> 5; matrix products, arithmetic and copies ran while one was open for 1% -> 3% of each run, Pallas kernels for 0% -> 7%
where the time goes in v1:
time: 685 us; the launch traced here: 682 us
  waiting for transfers between devices  531 us (78%)
  Pallas kernels  89.7 us (13%)
  local copies, waits for them, and re-layouts  21.8 us (3%)
  between operations  14.1 us (2%)
  starting transfers between devices  14 us (2%)
  other arithmetic  11.3 us (2%)
    psum x1, waiting for transfers between devices, on_device(): gram = lax.psum(gram, ('tri', 'colx', 'coly'))  276 us
    ppermute x3, waiting for transfers between devices, on_device(): pieces[d] = lax.ppermute(chunk(d), 'tri', ring(d))  141 us
    ppermute x3, waiting for transfers between devices, on_device(): results[d] = lax.ppermute(part, 'tri', ring(d)) if d else part  114 us
    pallas_call x4, Pallas kernels, correction_call(): pl.pallas_call(correction_kernel, grid_spec=pltpu.PrefetchScalarGridSpec(...  66.8 us
    pallas_call x1, Pallas kernels, gram_call(): pl.pallas_call(functools.partial(gram_kernel, scale, n, per), grid_spec=p...  22.9 us
  transfers between devices with their start and end apart: 7, of which 5 were waited for; matrix products, arithmetic and copies ran while one was open for 3% of the time, Pallas kernels for 7%

profile of v1, /device:TPU:0, one launch (start us, length us, event | category | flops | bytes accessed | tf_op | source)
XLA Modules:
  0.0 681.6 jit_solution(8629473098212370099)
XLA Ops:
  7.2 0.0 all-reduce.2.cloned.1.call-start
  7.2 0.0 copy-start.1
  7.3 6.6 constant_dynamic-slice_fusion
  13.8 3.1 collective-permute-start
  16.9 2.6 collective-permute-start.1
  19.5 1.3 collective-permute-start.2
  20.8 0.0 copy-done.1
  20.9 0.7 copy.6.where
  21.6 46.7 %collective-permute-done.refs_1_ = f32[432,1280]{1,0:T(8,128)} collective-permute-done((f32[432,1280]{1,0:T(8,128)}, f32[432,1280]{1,0:T(8,128)}, u32[]{:S(2)}, u32[]{:S(2)}) %collective-permute-start) | collective-permute-done | bytes 2211872 | tf_op jit(solution)/shard_map/ppermute | solution.py:159
  68.3 93.9 %collective-permute-done.1.refs_2_ = f32[432,1280]{1,0:T(8,128)} collective-permute-done((f32[432,1280]{1,0:T(8,128)}, f32[432,1280]{1,0:T(8,128)}, u32[]{:S(2)}, u32[]{:S(2)}) %collective-permute-start.1) | collective-permute-done | bytes 2211872 | tf_op jit(solution)/shard_map/ppermute | solution.py:159
  162.3 0.0 collective-permute-done.2.refs_3_
  162.3 22.9 %gram.1 = (f32[48,256,256]{2,1,0:T(8,128)}, bf16[20,432,256]{2,1,0:T(8,128)(2,1)}, bf16[20,432,256]{2,1,0:T(8,128)(2,1)}) custom-call(s32[48,2]{1,0:T(8,128)} %copy.6.where, f32[432,1280]{1,0:T(8,128)} %get-tuple-element.18.refs_0_, f32[432,1280]{1,0:T(8,128)} %collective-permute-done.refs_1_, f32[432,1280]{1,0:T(8,128)} %collective-permute-done.1.refs_2_, ...), custom_call_target="tpu_custom_call" | custom-call | flops 8153726976 | bytes 30277632 | tf_op jit(solution)/shard_map/gram/pallas_call | solution.py:62
  185.2 0.0 all-reduce.2.cloned.1.call-update
  185.2 0.7 copy.8.table
  185.9 276.4 %all-reduce.2.cloned.1.call-done.gram = f32[48,256,256]{2,1,0:T(8,128)} async-done(((f32[48,256,256]{2,1,0:T(8,128)}), f32[48,256,256]{2,1,0:T(8,128)}) %all-reduce.2.cloned.1.call-update) | async-done | bytes 12582928 | tf_op jit(solution)/shard_map/psum | solution.py:169
  462.3 16.0 %correction.5 = f32[432,1280]{1,0:T(8,128)} custom-call(s32[48,4]{1,0:T(8,128)} %copy.8.table, f32[48,256,256]{2,1,0:T(8,128)} %all-reduce.2.cloned.1.call-done.gram, bf16[20,432,256]{2,1,0:T(8,128)(2,1)} %get-tuple-element.6.high, bf16[20,432,256]{2,1,0:T(8,128)(2,1)} %get-tuple-element.7.low), custom_call_target="tpu_custom_call" | custom-call | flops 4076863488 | bytes 21430272 | tf_op jit(solution)/shard_map/correction/pallas_call | solution.py:121
  478.3 4.1 collective-permute-start.3
  482.4 0.7 copy.9.table
  483.1 15.2 %correction.6 = f32[432,1280]{1,0:T(8,128)} custom-call(s32[48,4]{1,0:T(8,128)} %copy.9.table, f32[48,256,256]{2,1,0:T(8,128)} %all-reduce.2.cloned.1.call-done.gram, bf16[20,432,256]{2,1,0:T(8,128)(2,1)} %get-tuple-element.6.high, bf16[20,432,256]{2,1,0:T(8,128)(2,1)} %get-tuple-element.7.low), custom_call_target="tpu_custom_call" | custom-call | flops 4076863488 | bytes 21430272 | tf_op jit(solution)/shard_map/correction/pallas_call | solution.py:121
  498.3 0.0 collective-permute-start.4
  498.3 7.6 %copy.12 = f32[1728,1280]{1,0:T(8,128)} copy(f32[1728,1280]{1,0:T(8,128)} %param.2) | data formatting | bytes 17694720
  505.9 0.7 copy.10.table
  506.6 0.7 copy.7.table
  507.3 17.0 %correction.7 = f32[432,1280]{1,0:T(8,128)} custom-call(s32[48,4]{1,0:T(8,128)} %copy.10.table, f32[48,256,256]{2,1,0:T(8,128)} %all-reduce.2.cloned.1.call-done.gram, bf16[20,432,256]{2,1,0:T(8,128)(2,1)} %get-tuple-element.6.high, bf16[20,432,256]{2,1,0:T(8,128)(2,1)} %get-tuple-element.7.low), custom_call_target="tpu_custom_call" | custom-call | flops 4076863488 | bytes 21430272 | tf_op jit(solution)/shard_map/correction/pallas_call | solution.py:121
  524.3 2.8 collective-permute-start.5
  527.1 18.6 %correction.4 = f32[432,1280]{1,0:T(8,128)} custom-call(s32[48,4]{1,0:T(8,128)} %copy.7.table, f32[48,256,256]{2,1,0:T(8,128)} %all-reduce.2.cloned.1.call-done.gram, bf16[20,432,256]{2,1,0:T(8,128)(2,1)} %get-tuple-element.6.high, bf16[20,432,256]{2,1,0:T(8,128)(2,1)} %get-tuple-element.7.low), custom_call_target="tpu_custom_call" | custom-call | flops 4076863488 | bytes 21430272 | tf_op jit(solution)/shard_map/correction/pallas_call | solution.py:121
  545.7 0.0 slice-start
  545.7 0.0 slice-start.1
  545.7 0.6 broadcast_in_dim.17
  546.3 0.0 slice-start.2
  546.3 4.3 subtract_dynamic-update-slice_fusion.3
  550.7 74.2 %collective-permute-done.3 = f32[432,1280]{1,0:T(8,128)S(1)} collective-permute-done((f32[432,1280]{1,0:T(8,128)}, f32[432,1280]{1,0:T(8,128)S(1)}, u32[]{:S(2)}, u32[]{:S(2)}) %collective-permute-start.3) | collective-permute-done | bytes 2211872 | tf_op jit(solution)/shard_map/ppermute | solution.py:179
  624.9 0.0 slice-done
  624.9 0.0 slice-done.1
  624.9 0.0 slice-done.2
  624.9 1.8 subtract_dynamic-update-slice_fusion.2
  626.7 0.0 collective-permute-done.4
  626.7 3.4 subtract_dynamic-update-slice_fusion.1
  630.1 39.3 %collective-permute-done.5 = f32[432,1280]{1,0:T(8,128)S(1)} collective-permute-done((f32[432,1280]{1,0:T(8,128)}, f32[432,1280]{1,0:T(8,128)S(1)}, u32[]{:S(2)}, u32[]{:S(2)}) %collective-permute-start.5) | collective-permute-done | bytes 2211872 | tf_op jit(solution)/shard_map/ppermute | solution.py:179
  669.4 1.8 subtract_dynamic-update-slice_fusion
  671.2 0.0 copy-start
  671.2 3.5 copy-done
  (6 shorter events, 0.1 us)
Async XLA Ops:
  7.2 455.1 %all-reduce.2.cloned.1.call-start = ((), (), s32[]{:S(2)}) async-start(), calls=%async_computation | async-start | bytes 25165824 | tf_op jit(solution)/shard_map/psum | solution.py:169
  7.2 13.6 %copy-start.1 = (s32[48,3]{0,1:T(4,128)S(1)}, s32[48,3]{0,1:T(4,128)}, u32[]{:S(2)}) copy-start(s32[48,3]{0,1:T(4,128)} %param.3) | copy-start | bytes 1732
  13.8 54.5 %collective-permute-start = (f32[432,1280]{1,0:T(8,128)}, f32[432,1280]{1,0:T(8,128)}, u32[]{:S(2)}, u32[]{:S(2)}) collective-permute-start(f32[432,1280]{1,0:T(8,128)} %get-tuple-element.17), channel_id=1, source_target_pairs={{0,8},{8,16},{16,24},{24,0},{1,9},{9,17},{17,25},{25,1},{2,10},{10... | collective-permute-start | bytes 6635528 | tf_op jit(solution)/shard_map/ppermute | solution.py:159
  16.9 145.4 %collective-permute-start.1 = (f32[432,1280]{1,0:T(8,128)}, f32[432,1280]{1,0:T(8,128)}, u32[]{:S(2)}, u32[]{:S(2)}) collective-permute-start(f32[432,1280]{1,0:T(8,128)} %get-tuple-element.16), channel_id=1, source_target_pairs={{0,16},{8,24},{16,0},{24,8},{1,17},{9,25},{17,1},{25,9},{2,18},{10... | collective-permute-start | bytes 6635528 | tf_op jit(solution)/shard_map/ppermute | solution.py:159
  19.5 142.8 %collective-permute-start.2 = (f32[432,1280]{1,0:T(8,128)S(1)}, f32[432,1280]{1,0:T(8,128)}, u32[]{:S(2)}, u32[]{:S(2)}) collective-permute-start(f32[432,1280]{1,0:T(8,128)S(1)} %get-tuple-element.15), channel_id=1, source_target_pairs={{0,24},{8,0},{16,8},{24,16},{1,25},{9,1},{17,9},{25,17},{2,26},{10... | collective-permute-start | bytes 6635528 | tf_op jit(solution)/shard_map/ppermute | solution.py:159
  478.3 146.6 %collective-permute-start.3 = (f32[432,1280]{1,0:T(8,128)}, f32[432,1280]{1,0:T(8,128)S(1)}, u32[]{:S(2)}, u32[]{:S(2)}) collective-permute-start(f32[432,1280]{1,0:T(8,128)} %correction.5), channel_id=1, source_target_pairs={{0,16},{8,24},{16,0},{24,8},{1,17},{9,25},{17,1},{25,9},{2,18},{10... | collective-permute-start | bytes 6635528 | tf_op jit(solution)/shard_map/ppermute | solution.py:179
  498.3 128.4 %collective-permute-start.4 = (f32[432,1280]{1,0:T(8,128)}, f32[432,1280]{1,0:T(8,128)}, u32[]{:S(2)}, u32[]{:S(2)}) collective-permute-start(f32[432,1280]{1,0:T(8,128)} %correction.6), channel_id=1, source_target_pairs={{0,8},{8,16},{16,24},{24,0},{1,9},{9,17},{17,25},{25,1},{2,10},{10... | collective-permute-start | bytes 6635528 | tf_op jit(solution)/shard_map/ppermute | solution.py:179
  524.3 145.1 %collective-permute-start.5 = (f32[432,1280]{1,0:T(8,128)}, f32[432,1280]{1,0:T(8,128)S(1)}, u32[]{:S(2)}, u32[]{:S(2)}) collective-permute-start(f32[432,1280]{1,0:T(8,128)} %correction.7), channel_id=1, source_target_pairs={{0,24},{8,0},{16,8},{24,16},{1,25},{9,1},{17,9},{25,17},{2,26},{10... | collective-permute-start | bytes 6635528 | tf_op jit(solution)/shard_map/ppermute | solution.py:179
  545.7 79.2 %slice-start = ((s8[8847360]{0:T(1024)(128)(4,1)}), s8[4194304]{0:T(1024)(128)(4,1)S(1)}, s32[]{:S(2)}) async-start(s8[8847360]{0:T(1024)(128)(4,1)} %bitcast), calls=%async_computation.1 | async-start | bytes 8388608
  545.7 79.2 %slice-start.1 = ((s8[8847360]{0:T(1024)(128)(4,1)}), s8[4194304]{0:T(1024)(128)(4,1)S(1)}, s32[]{:S(2)}) async-start(s8[8847360]{0:T(1024)(128)(4,1)} %bitcast), calls=%async_computation.2 | async-start | bytes 8388608
  546.3 78.6 %slice-start.2 = ((s8[8847360]{0:T(1024)(128)(4,1)}), s8[458752]{0:T(1024)(128)(4,1)S(1)}, s32[]{:S(2)}) async-start(s8[8847360]{0:T(1024)(128)(4,1)} %bitcast), calls=%async_computation.3 | async-start | bytes 917504
  671.2 3.5 copy-start
Sparse Core Ops, SparseCore 0:
  185.3 276.9 all-reduce.1

commit v2 on v1

v2 whole, which is shorter than its diff:
```python
import functools
import math

import jax
import jax.numpy as jnp
from jax import lax
from jax.experimental import pallas as pl
from jax.experimental.pallas import tpu as pltpu
from jax.sharding import PartitionSpec as P


PANEL = 256
VMEM_LIMIT = 56 * 1024 * 1024
GROUP = 4


def split(x):
    high = x.astype(jnp.bfloat16)
    low = (x - high.astype(jnp.float32)).astype(jnp.bfloat16)
    return high, low


def product(left, right, dims):
    (lh, ll), (rh, rl) = left, right

    def dot(a, b):
        return lax.dot_general(a, b, (dims, ((), ())), preferred_element_type=jnp.float32)

    return dot(lh, rh) + (dot(lh, rl) + dot(ll, rh))


def load_kernel(n, per, *refs):
    pieces = refs[:n]
    high, low, turned_high, turned_low = refs[n:]
    for d in range(n):
        for s in range(per):
            x = pieces[d][:, s * PANEL : (s + 1) * PANEL]
            high[d * per + s], low[d * per + s] = split(x)
            turned_high[d * per + s], turned_low[d * per + s] = split(x.T)


def gram_first_kernel(scale, n, per, where, *refs):
    pieces = refs[:n]
    gram, kept = refs[n], refs[n + 1 :]

    @pl.when(pl.program_id(0) == 0)
    def _():
        load_kernel(n, per, *pieces, *kept)

    gram_kernel(scale, where, *kept, gram)


def gram_kernel(scale, where, high, low, turned_high, turned_low, gram):
    for t in range(GROUP):
        k = pl.program_id(0) * GROUP + t
        i, j = where[k, 0], where[k, 1]
        gram[t] = scale * product((turned_high[i], turned_low[i]), (high[j], low[j]), ((1,), (0,)))


def still(shape):
    return pl.BlockSpec(shape, lambda k, w: (0,) * len(shape), pipeline_mode=pl.Buffered(1))


def gram_call(where, arrays, scale, first):
    count = where.shape[0]
    n = len(arrays)
    if first:
        rows, width = arrays[0].shape
        slots = n * width // PANEL
    else:
        slots, rows, _ = arrays[0].shape
    kept = [(slots, rows, PANEL)] * 2 + [(slots, PANEL, rows)] * 2
    gram_spec = pl.BlockSpec((GROUP, PANEL, PANEL), lambda k, w: (k, 0, 0))
    gram_shape = jax.ShapeDtypeStruct((count, PANEL, PANEL), jnp.float32)
    return pl.pallas_call(
        functools.partial(gram_first_kernel, scale, n, slots // n)
        if first
        else functools.partial(gram_kernel, scale),
        grid_spec=pltpu.PrefetchScalarGridSpec(
            num_scalar_prefetch=1,
            grid=(count // GROUP,),
            in_specs=[still(a.shape) for a in arrays],
            out_specs=[gram_spec] + [still(shape) for shape in kept] if first else gram_spec,
        ),
        out_shape=[gram_shape] + [jax.ShapeDtypeStruct(shape, jnp.bfloat16) for shape in kept]
        if first
        else gram_shape,
        compiler_params=pltpu.CompilerParams(
            dimension_semantics=("arbitrary",), vmem_limit_bytes=VMEM_LIMIT
        ),
        cost_estimate=pl.CostEstimate(
            flops=6 * count * PANEL * PANEL * rows,
            bytes_accessed=8 * slots * rows * PANEL + 4 * count * PANEL * PANEL,
            transcendentals=0,
        ),
        name="gram_first" if first else "gram",
    )(where, *arrays)


def correction_kernel(parts, raw, table, *refs):
    grams = refs[:parts]
    step = pl.program_id(0)
    if raw:
        out, high, low = refs[parts + raw :]

        @pl.when(step == 0)
        def _():
            per = high.shape[0] // raw
            for d in range(raw):
                for s in range(per):
                    x = refs[parts + d][:, s * PANEL : (s + 1) * PANEL]
                    high[d * per + s], low[d * per + s] = split(x)

    else:
        high, low, out = refs[parts:]
    size = grams[0].shape[0]
    steps = pl.num_programs(0)

    @pl.when(step == 0)
    def _():
        out[...] = jnp.zeros_like(out)

    for part in range(parts):
        gram = grams[part]

        def one(t, carry):
            k = (part * steps + step) * size + t
            i, j, first, second = table[k, 0], table[k, 1], table[k, 2], table[k, 3]

            @pl.when(first >= 0)
            def _():
                at = pl.ds(pl.multiple_of(first * PANEL, PANEL), PANEL)
                out[:, at] += product((high[j], low[j]), split(gram[t]), ((1,), (1,)))

            @pl.when(second >= 0)
            def _():
                at = pl.ds(pl.multiple_of(second * PANEL, PANEL), PANEL)
                out[:, at] += product((high[i], low[i]), split(gram[t]), ((1,), (0,)))

            return carry

        lax.fori_loop(0, size, one, 0)


BLOCK = 2


def correction_call(table, grams, arrays, rows, per):
    raw = arrays[0].ndim == 2
    if raw:
        slots = len(arrays) * per
        specs, scratch = [still(a.shape) for a in arrays], [pltpu.VMEM((slots, rows, PANEL), jnp.bfloat16)] * 2
    else:
        slots = arrays[0].shape[0]
        specs, scratch = [still((slots, rows, PANEL))] * 2, []
    count = grams[0].shape[0]
    return pl.pallas_call(
        functools.partial(correction_kernel, len(grams), len(arrays) if raw else 0),
        grid_spec=pltpu.PrefetchScalarGridSpec(
            num_scalar_prefetch=1,
            grid=(count // BLOCK,),
            in_specs=[pl.BlockSpec((BLOCK, PANEL, PANEL), lambda k, w: (k, 0, 0))] * len(grams)
            + specs,
            out_specs=still((rows, per * PANEL)),
            scratch_shapes=scratch,
        ),
        out_shape=jax.ShapeDtypeStruct((rows, per * PANEL), jnp.float32),
        compiler_params=pltpu.CompilerParams(
            dimension_semantics=("arbitrary",), vmem_limit_bytes=VMEM_LIMIT
        ),
        cost_estimate=pl.CostEstimate(
            flops=3 * table.shape[0] * PANEL * PANEL * rows,
            bytes_accessed=4 * slots * rows * PANEL + 4 * table.shape[0] * PANEL * PANEL,
            transcendentals=0,
        ),
        name="correction",
    )(table, *grams, *arrays)


def place_kernel(at, part, weight, *refs):
    correction, updated = refs[-2:]
    correction[...] = part[...]
    updated[...] = 1.5 * weight[...] - 0.5 * part[...]


def place_call(at, part, weight, earlier, block):
    size, width = part.shape
    here = pl.BlockSpec((block, width), lambda g, a: (g, 0))
    there = pl.BlockSpec((block, width), lambda g, a: (a[0] + g, 0))
    return pl.pallas_call(
        place_kernel,
        grid_spec=pltpu.PrefetchScalarGridSpec(
            num_scalar_prefetch=1,
            grid=(size // block,),
            in_specs=[here, there] + [pl.BlockSpec(memory_space=pl.ANY)] * len(earlier),
            out_specs=[there, there],
        ),
        out_shape=[jax.ShapeDtypeStruct(weight.shape, weight.dtype)] * 2,
        input_output_aliases={3: 0, 4: 1} if earlier else {},
        compiler_params=pltpu.CompilerParams(dimension_semantics=("arbitrary",)),
        cost_estimate=pl.CostEstimate(flops=3 * size * width, bytes_accessed=16 * size * width, transcendentals=0),
        name="place",
    )(at[None] // block, part, weight, *earlier)


together = lax.optimization_barrier


def flip(value, dim):
    axis, mask = dim
    pairs = [(s, s ^ mask) for s in range(lax.axis_size(axis))]
    return lax.ppermute(value, axis, pairs)


def side(dim):
    axis, mask = dim
    return lax.axis_index(axis) // mask % 2


def bits_of(axis, lowest=1):
    size, mask, found = lax.axis_size(axis), lowest, []
    while mask < size:
        found.append((axis, mask))
        mask *= 2
    return found[::-1]


def cut(terms, start, rows):
    return sum(lax.dynamic_slice_in_dim(t, base + start, rows, 0) for base, t in terms)


def whole_sum(kept, got, orders):
    colours, rows = len(orders), kept.shape[0] // len(orders)
    terms = [[(c * rows, t) for t in (kept, got)] for c in range(colours)]
    for dims in zip(*orders):
        rows //= 2
        sides = [side(dim) for dim in dims]
        sent = together([cut(t, (1 - b) * rows, rows) for t, b in zip(terms, sides)])
        came = [flip(v, dim) for v, dim in zip(sent, dims)]
        mine = [cut(t, b * rows, rows) for t, b in zip(terms, sides)]
        terms = [[(0, a), (0, b)] for a, b in zip(mine, together(came))]
    done = together([a + b for (_, a), (_, b) in terms])
    for dims in list(zip(*orders))[:0:-1]:
        came = together([flip(v, dim) for v, dim in zip(done, dims)])
        joined = []
        for v, w, dim in zip(done, came, dims):
            if rows % PANEL:
                b = side(dim)
                both = lax.dynamic_update_slice_in_dim(jnp.zeros_like(jnp.concatenate([v, w])), v, b * rows, 0)
                joined.append(lax.dynamic_update_slice_in_dim(both, w, (1 - b) * rows, 0))
            else:
                joined.append(jnp.concatenate([v, w]))
        rows *= 2
        done = together(joined)
    came = [flip(v, dim) for v, dim in zip(done, [order[0] for order in orders])]
    return done, came


def tile_at(orders, core, count):
    places = jnp.arange(count, dtype=jnp.int32)
    per = count // 2 // len(orders)
    buffer, place = places // (count // 4), places % (count // 4)
    colour, spot = place // (per // 2), place % (per // 2)
    half = jnp.stack([side(order[0]) for order in orders])[colour]
    tile = half ^ (buffer % 2)
    unit, level = per // 2, 1
    while unit % 2 == 0:
        unit //= 2
        other = jnp.stack([side(order[level]) for order in orders])[colour]
        tile = tile * 2 + (spot // unit % 2 ^ other)
        level += 1
    tile = tile * unit + spot % unit
    return (core ^ (buffer // 2)) * (count // 2) + colour * per + tile


def on_device(columns, weight, tiles):
    n = lax.axis_size("tri")
    z = lax.axis_index("tri")
    local, width = weight.shape
    per = width // PANEL
    count = tiles.shape[0]
    rows = -(-local // (n * 16)) * 16
    padded = jnp.pad(weight, ((0, n * rows - local), (0, 0))) if n * rows != local else weight

    core_dim = ("colx", 1)
    along_x, along_y, along_z = bits_of("colx", 2), bits_of("coly"), bits_of("tri")
    near, far = along_z[1:], along_z[:1]
    orders = [along_x + along_y + near + far, along_y + near + along_x + far, near + along_x + along_y + far]
    core = side(core_dim)

    def place(panel):
        return (z ^ (panel // per)) * per + panel % per

    def target(panel, d):
        return jnp.where(panel // per == z ^ d, panel % per, -1)

    first, second = tiles[:, 0], tiles[:, 1]
    where = jnp.stack([place(first), place(second)], axis=1)
    half = count // 2
    where_sent = lax.dynamic_slice_in_dim(where, (1 - core) * half, half, 0)
    where_kept = lax.dynamic_slice_in_dim(where, core * half, half, 0)
    stood = tiles[tile_at(orders, core, count)]
    first, second = stood[:, 0], stood[:, 1]
    tables = []
    for d in range(n):
        onto = jnp.where(first == second, -1, target(second, d))
        tables.append(jnp.stack([place(first), place(second), target(first, d), onto], axis=1))

    order = list(range(n - 1, 0, -1))
    pieces = [None] * n
    source = padded
    for d in order:
        chunk = lax.dynamic_slice_in_dim(source, (z ^ d) * rows, rows, 0)
        source, chunk = together((source, chunk))
        pieces[d] = flip(chunk, ("tri", d))
    pieces[0] = lax.dynamic_slice_in_dim(source, z * rows, rows, 0)

    top = n // 2
    more = rows // 3 // 16 * 16
    less = rows - more
    mirrored = []
    if more:
        for d in range(n):
            chunk = lax.dynamic_slice_in_dim(source, (z ^ d ^ top) * rows + less, more, 0)
            source, chunk = together((source, chunk))
            mirrored.append(chunk)
        pieces, mirrored = together((pieces, mirrored))
        mirrored = [flip(chunk, ("tri", d)) if d else chunk for d, chunk in enumerate(mirrored)]

    sent, *panels = gram_call(where_sent, pieces, 1.0 / columns, True)
    got = flip(sent, core_dim)

    kept = gram_call(where_kept, panels, 1.0 / columns, False)
    here, there = whole_sum(kept.reshape(half * PANEL, PANEL), got.reshape(half * PANEL, PANEL), orders)
    here = jnp.concatenate(here)
    here_other = flip(here, core_dim)
    there = jnp.concatenate(there)
    there_other = flip(there, core_dim)
    grams = [g.reshape(count // 4, PANEL, PANEL) for g in (here, there, here_other, there_other)]

    ready = []
    for d in range(n - 1, -1, -1):
        found = [((z ^ d) * rows, correction_call(tables[d], grams, panels[:2], less if d >= top else rows, per))]
        if more and d < top:
            found.append(((z ^ d ^ top) * rows + less, correction_call(tables[d], grams, mirrored, more, per)))
        if d:
            ready += [(at, flip(part, ("tri", d))) for at, part in found]
        else:
            ready = found + ready

    block = math.gcd(rows, more)
    placed = ()
    for at, part in ready:
        placed = place_call(at, part, padded, placed, block)
    correction, updated = placed
    return correction[:local], updated[:local]


def solution(mesh):
    spec = P(("colx", "coly"), "tri")

    def step(weight, tiles):
        body = jax.shard_map(
            functools.partial(on_device, weight.shape[0]),
            mesh=mesh,
            in_specs=(spec, P()),
            out_specs=(spec, spec),
            check_vma=False,
        )
        return body(weight, tiles)

    return step
```

time: 685 us -> 624 us (0.911)
  waiting for transfers between devices: 531 us -> 342 us
  starting transfers between devices: 14 us -> 86.9 us
  Pallas kernels: 89.7 us -> 147 us
  between operations: 14.1 us -> 0.97 us
  other arithmetic: 11.3 us -> 19.8 us
    psum x1 -> x0, waiting for transfers between devices: 276 us -> none  [on_device(): gram = lax.psum(gram, ('tri', 'colx', 'coly'))]
    ppermute x6 -> x37, waiting for transfers between devices: 254 us -> 342 us  [flip(): return lax.ppermute(value, axis, pairs)]
    ppermute x6 -> x37, starting transfers between devices: 13.9 us -> 86.9 us  [flip(): return lax.ppermute(value, axis, pairs)]
    pallas_call x5 -> x14, Pallas kernels: 89.7 us -> 147 us  [the longest x6 91.6 us: correction_call(): pl.pallas_call(functools.partial(correction_kernel, len(grams), len(array...]
    add x0 -> x14, other arithmetic: none -> 16.8 us  [the longest x10 16.6 us: cut(): sum((lax.dynamic_slice_in_dim(t, base + start, rows, 0) for base, t in te...]
    dynamic_slice x1 -> x8, local copies, waits for them, and re-layouts: 6.59 us -> 19.4 us  [the longest x4 8.23 us: on_device(): lax.dynamic_slice_in_dim(source, (z ^ d ^ top) * rows + less, more, 0)]
    dynamic_update_slice x4 -> x0, other arithmetic: 11.3 us -> none  [on_device(): lax.dynamic_update_slice_in_dim(updated, 1.5 * old - 0.5 * results[d], at...]
  transfers between devices with their start and end apart: 7 -> 37, of which waited for: 5 -> 28; matrix products, arithmetic and copies ran while one was open for 3% -> 2% of each run, Pallas kernels for 7% -> 20%
where the time goes in v2:
time: 624 us; the launch traced here: 622 us
  waiting for transfers between devices  342 us (55%)
  Pallas kernels  147 us (24%)
  starting transfers between devices  86.9 us (14%)
  local copies, waits for them, and re-layouts  25.6 us (4%)
  other arithmetic  19.8 us (3%)
    ppermute x37, waiting for transfers between devices, flip(): return lax.ppermute(value, axis, pairs)  342 us
    pallas_call x6, Pallas kernels, correction_call(): pl.pallas_call(functools.partial(correction_kernel, len(grams), len(array...  91.6 us
    ppermute x37, starting transfers between devices, flip(): return lax.ppermute(value, axis, pairs)  86.9 us
    pallas_call x2, Pallas kernels, gram_call(): pl.pallas_call(functools.partial(gram_first_kernel, scale, n, slots // n)...  34.2 us
    pallas_call x6, Pallas kernels, place_call(): pl.pallas_call(place_kernel, grid_spec=pltpu.PrefetchScalarGridSpec(num_s...  21.4 us
    add x10, other arithmetic, cut(): sum((lax.dynamic_slice_in_dim(t, base + start, rows, 0) for base, t in te...  16.6 us
  transfers between devices with their start and end apart: 37, of which 28 were waited for; matrix products, arithmetic and copies ran while one was open for 2% of the time, Pallas kernels for 20%

profile of v2, /device:TPU:0, one launch (start us, length us, event | category | flops | bytes accessed | tf_op | source)
XLA Modules:
  0.0 622.2 jit_solution(4110193791469026743)
XLA Ops:
  2.4 3.2 constant_dynamic-slice_fusion.6
  5.6 3.1 constant_dynamic-slice_fusion.5
  8.7 3.1 collective-permute-start
  11.8 2.6 collective-permute-start.1
  18.6 2.1 constant_dynamic-slice_fusion.1
  24.3 3.1 constant_dynamic-slice_fusion.4.refs_0_
  27.5 79.4 %collective-permute-done.refs_1_ = f32[432,1280]{1,0:T(8,128)} collective-permute-done((f32[432,1280]{1,0:T(8,128)}, f32[432,1280]{1,0:T(8,128)}, u32[]{:S(2)}, u32[]{:S(2)}) %collective-permute-start) | collective-permute-done | bytes 2211872 | tf_op jit(solution)/shard_map/ppermute | solution.py:212
  106.8 51.9 %collective-permute-done.1.refs_2_ = f32[432,1280]{1,0:T(8,128)} collective-permute-done((f32[432,1280]{1,0:T(8,128)}, f32[432,1280]{1,0:T(8,128)}, u32[]{:S(2)}, u32[]{:S(2)}) %collective-permute-start.1) | collective-permute-done | bytes 2211872 | tf_op jit(solution)/shard_map/ppermute | solution.py:212
  158.8 19.7 %gram_first.1 = (f32[24,256,256]{2,1,0:T(8,128)}, bf16[20,432,256]{2,1,0:T(8,128)(2,1)}, bf16[20,432,256]{2,1,0:T(8,128)(2,1)}, bf16[20,256,432]{2,1,0:T(8,128)(2,1)}, bf16[20,256,432]{2,1,0:T(8,128)(2,1)}) custom-call(s32[24,2]{1,0:T(8,128)} %get-tuple-element.187.where, f32[432,1280]{1,0:T(8,128)} %constant_dynamic-slice_fusion.4.refs_0_, ...), custom_call_target="tpu_custom_call" | custom-call | flops 4076863488 | bytes 23986176 | tf_op jit(solution)/shard_map/gram_first/pallas_call | solution.py:75
  178.4 14.6 %gram.1 = f32[24,256,256]{2,1,0:T(8,128)} custom-call(s32[24,2]{1,0:T(8,128)} %get-tuple-element.186.where, bf16[20,432,256]{2,1,0:T(8,128)(2,1)} %get-tuple-element.100.high.refs_4_, bf16[20,432,256]{2,1,0:T(8,128)(2,1)} %get-tuple-element.101.low.refs_5_, bf16[20,256,432]{2,1,0:T(8,128)(2,1)} %get-tuple-element.102.turned_high, ...), custom_call_target="tpu_custom_call" | custom-call | flops 4076863488 | bytes 23986176 | tf_op jit(solution)/shard_map/gram/pallas_call | solution.py:75
  193.0 6.9 %dynamic-slice_add_fusion = (f32[1024,256]{1,0:T(8,128)S(1)}, f32[1024,256]{1,0:T(8,128)S(1)}, f32[1024,256]{1,0:T(8,128)}, f32[1024,256]{1,0:T(8,128)}, f32[1024,256]{1,0:T(8,128)}, /*index=5*/f32[1024,256]{1,0:T(8,128)S(1)}) fusion(f32[6144,256]{1,0:T(8,128)} %bitcast.3, s32[]{:T(128)S(6)} %select_n.589, f32[6144,256]{1,0:T(8,128)} %bitcast.42, ...), kind=kLoop, calls=%fused_computation.4 | loop fusion | flops 1572864 | bytes 18874392 | tf_op jit(solution)/shard_map/add | solution.py:229
  202.9 46.6 %collective-permute-start.6 = (f32[1024,256]{1,0:T(8,128)}, f32[1024,256]{1,0:T(8,128)}, u32[]{:S(2)}, u32[]{:S(2)}) collective-permute-start(f32[1024,256]{1,0:T(8,128)} %get-tuple-element.107), channel_id=1, source_target_pairs={{0,8},{8,0},{16,24},{24,16},{1,9},{9,1},{17,25},{25,17},{2,10},{10... | collective-permute-start | bytes 3145736 | tf_op jit(solution)/shard_map/ppermute | solution.py:212
  249.5 23.5 %collective-permute-done.6 = f32[1024,256]{1,0:T(8,128)} collective-permute-done((f32[1024,256]{1,0:T(8,128)}, f32[1024,256]{1,0:T(8,128)}, u32[]{:S(2)}, u32[]{:S(2)}) %collective-permute-start.6) | collective-permute-done | bytes 1048608 | tf_op jit(solution)/shard_map/ppermute | solution.py:212
  273.1 2.3 dynamic-slice_add_fusion.6
  275.4 2.2 dynamic-slice_add_fusion.11
  277.5 2.1 dynamic-slice_add_fusion.7
  282.4 10.6 %collective-permute-done.7 = f32[512,256]{1,0:T(8,128)S(1)} collective-permute-done((f32[512,256]{1,0:T(8,128)}, f32[512,256]{1,0:T(8,128)S(1)}, u32[]{:S(2)}, u32[]{:S(2)}) %collective-permute-start.7) | collective-permute-done | bytes 524320 | tf_op jit(solution)/shard_map/ppermute | solution.py:212
  300.2 3.8 collective-permute-done.10
  305.3 2.4 collective-permute-start.13
  308.3 2.3 collective-permute-start.15
  310.6 7.1 %collective-permute-done.13 = f32[128,256]{1,0:T(8,128)S(1)} collective-permute-done((f32[128,256]{1,0:T(8,128)S(1)}, f32[128,256]{1,0:T(8,128)S(1)}, u32[]{:S(2)}, u32[]{:S(2)}) %collective-permute-start.13) | collective-permute-done | bytes 131104 | tf_op jit(solution)/shard_map/ppermute | solution.py:212
  317.7 2.8 collective-permute-done.14
  322.8 3.0 collective-permute-start.17
  325.9 11.1 %collective-permute-done.16 = f32[128,256]{1,0:T(8,128)S(1)} collective-permute-done((f32[128,256]{1,0:T(8,128)S(1)}, f32[128,256]{1,0:T(8,128)S(1)}, u32[]{:S(2)}, u32[]{:S(2)}) %collective-permute-start.16) | collective-permute-done | bytes 131104 | tf_op jit(solution)/shard_map/ppermute | solution.py:212
  337.0 2.8 collective-permute-done.17
  339.9 2.6 collective-permute-done.18
  344.9 5.8 collective-permute-done.19
  355.2 9.5 %collective-permute-done.22 = f32[512,256]{1,0:T(8,128)S(1)} collective-permute-done((f32[512,256]{1,0:T(8,128)S(1)}, f32[512,256]{1,0:T(8,128)S(1)}, u32[]{:S(2)}, u32[]{:S(2)}) %collective-permute-start.22) | collective-permute-done | bytes 524320 | tf_op jit(solution)/shard_map/ppermute | solution.py:212
  369.5 19.6 %collective-permute-done.25 = f32[1024,256]{1,0:T(8,128)S(1)} collective-permute-done((f32[1024,256]{1,0:T(8,128)S(1)}, f32[1024,256]{1,0:T(8,128)S(1)}, u32[]{:S(2)}, u32[]{:S(2)}) %collective-permute-start.25) | collective-permute-done | bytes 1048608 | tf_op jit(solution)/shard_map/ppermute | solution.py:212
  393.0 2.9 collective-permute-done.29
  397.7 17.4 %correction.7 = f32[432,1280]{1,0:T(8,128)} custom-call(s32[48,4]{1,0:T(8,128)} %get-tuple-element.193.table, f32[12,256,256]{2,1,0:T(8,128)} %bitcast.24, f32[12,256,256]{2,1,0:T(8,128)} %bitcast.18, f32[12,256,256]{2,1,0:T(8,128)} %bitcast.30, f32[12,256,256]{2,1,0:T(8,128)} %bitcast.36, bf16[20,432,256]{2,1,0:T(8,128)(2,1)} %get-tuple-element.100.high.refs_4_, ...), custom_call_target="tpu_custom_call" | custom-call | flops 4076863488 | bytes 21430272 | tf_op jit(solution)/shard_map/correction/pallas_call | solution.py:157
  415.1 2.3 collective-permute-start.34
  417.4 2.4 collective-permute-start.32
  419.8 14.5 %correction.9 = f32[288,1280]{1,0:T(8,128)} custom-call(s32[48,4]{1,0:T(8,128)} %get-tuple-element.191.table, f32[12,256,256]{2,1,0:T(8,128)} %bitcast.25, f32[12,256,256]{2,1,0:T(8,128)} %bitcast.19, f32[12,256,256]{2,1,0:T(8,128)} %bitcast.31, f32[12,256,256]{2,1,0:T(8,128)} %bitcast.37, bf16[20,432,256]{2,1,0:T(8,128)(2,1)} %get-tuple-element.100.high.refs_4_, ...), custom_call_target="tpu_custom_call" | custom-call | flops 2717908992 | bytes 18481152 | tf_op jit(solution)/shard_map/correction/pallas_call | solution.py:157
  434.3 2.7 collective-permute-start.36
  437.0 13.2 %correction.8 = f32[288,1280]{1,0:T(8,128)} custom-call(s32[48,4]{1,0:T(8,128)} %get-tuple-element.192.table, f32[12,256,256]{2,1,0:T(8,128)} %bitcast.26, f32[12,256,256]{2,1,0:T(8,128)} %bitcast.20, f32[12,256,256]{2,1,0:T(8,128)} %bitcast.32, f32[12,256,256]{2,1,0:T(8,128)} %bitcast.38, bf16[20,432,256]{2,1,0:T(8,128)(2,1)} %get-tuple-element.100.high.refs_4_, ...), custom_call_target="tpu_custom_call" | custom-call | flops 2717908992 | bytes 18481152 | tf_op jit(solution)/shard_map/correction/pallas_call | solution.py:157
  451.8 30.1 %collective-permute-done.31.refs_6_ = f32[144,1280]{1,0:T(8,128)S(1)} collective-permute-done((f32[144,1280]{1,0:T(8,128)S(1)}, f32[144,1280]{1,0:T(8,128)S(1)}, u32[]{:S(2)}, u32[]{:S(2)}) %collective-permute-start.31) | collective-permute-done | bytes 737312 | tf_op jit(solution)/shard_map/ppermute | solution.py:212
  481.9 16.2 %collective-permute-done.32.refs_7_ = f32[144,1280]{1,0:T(8,128)S(1)} collective-permute-done((f32[144,1280]{1,0:T(8,128)}, f32[144,1280]{1,0:T(8,128)S(1)}, u32[]{:S(2)}, u32[]{:S(2)}) %collective-permute-start.32) | collective-permute-done | bytes 737312 | tf_op jit(solution)/shard_map/ppermute | solution.py:212
  499.0 13.4 %correction.6 = f32[144,1280]{1,0:T(8,128)} custom-call(s32[48,4]{1,0:T(8,128)} %get-tuple-element.193.table, f32[12,256,256]{2,1,0:T(8,128)} %bitcast.27, f32[12,256,256]{2,1,0:T(8,128)} %bitcast.21, f32[12,256,256]{2,1,0:T(8,128)} %bitcast.33, f32[12,256,256]{2,1,0:T(8,128)} %bitcast.39, f32[144,1280]{1,0:T(8,128)} %constant_dynamic-slice_fusion.3.refs_4_, ...), custom_call_target="tpu_custom_call" | custom-call | flops 1358954496 | bytes 15532032 | tf_op jit(solution)/shard_map/correction/pallas_call | solution.py:157
  512.5 18.6 %correction.11.part = f32[432,1280]{1,0:T(8,128)} custom-call(s32[48,4]{1,0:T(8,128)} %get-tuple-element.164.table, f32[12,256,256]{2,1,0:T(8,128)} %bitcast.28, f32[12,256,256]{2,1,0:T(8,128)} %bitcast.22, f32[12,256,256]{2,1,0:T(8,128)} %bitcast.34, f32[12,256,256]{2,1,0:T(8,128)} %bitcast.40, bf16[20,432,256]{2,1,0:T(8,128)(2,1)} %get-tuple-element.100.high.refs_4_, ...), custom_call_target="tpu_custom_call" | custom-call | flops 4076863488 | bytes 21430272 | tf_op jit(solution)/shard_map/correction/pallas_call | solution.py:157
  531.0 5.2 place.6
  536.2 14.5 %correction.10.part = f32[144,1280]{1,0:T(8,128)} custom-call(s32[48,4]{1,0:T(8,128)} %get-tuple-element.164.table, f32[12,256,256]{2,1,0:T(8,128)} %bitcast.29, f32[12,256,256]{2,1,0:T(8,128)} %bitcast.23, f32[12,256,256]{2,1,0:T(8,128)} %bitcast.35, f32[12,256,256]{2,1,0:T(8,128)} %bitcast.41, f32[144,1280]{1,0:T(8,128)} %constant_dynamic-slice_fusion.3.refs_4_, ...), custom_call_target="tpu_custom_call" | custom-call | flops 1358954496 | bytes 15532032 | tf_op jit(solution)/shard_map/correction/pallas_call | solution.py:157
  550.7 2.5 place.7
  554.4 3.0 place.8
  557.4 52.9 %collective-permute-done.35.part = f32[288,1280]{1,0:T(8,128)S(1)} collective-permute-done((f32[288,1280]{1,0:T(8,128)}, f32[288,1280]{1,0:T(8,128)S(1)}, u32[]{:S(2)}, u32[]{:S(2)}) %collective-permute-start.35) | collective-permute-done | bytes 1474592 | tf_op jit(solution)/shard_map/ppermute | solution.py:212
  611.4 3.0 place.9
  614.5 5.2 place.10
  619.7 2.5 place.11
  (119 shorter events, 48.6 us)
Async XLA Ops:
  5.6 8.8 %copy-start.13 = (s32[48,3]{0,1:T(4,128)S(1)}, s32[48,3]{0,1:T(4,128)}, u32[]{:S(2)}) copy-start(s32[48,3]{0,1:T(4,128)} %param.3) | copy-start | bytes 1732
  8.7 98.1 %collective-permute-start = (f32[432,1280]{1,0:T(8,128)}, f32[432,1280]{1,0:T(8,128)}, u32[]{:S(2)}, u32[]{:S(2)}) collective-permute-start(f32[432,1280]{1,0:T(8,128)} %constant_dynamic-slice_fusion.5), channel_id=1, source_target_pairs={{0,8},{8,0},{16,24},{24,16},{1,9},{9,1},{17,25},{25,17},{2,10},{10... | collective-permute-start | bytes 6635528 | tf_op jit(solution)/shard_map/ppermute | solution.py:212
  11.8 147.0 %collective-permute-start.1 = (f32[432,1280]{1,0:T(8,128)}, f32[432,1280]{1,0:T(8,128)}, u32[]{:S(2)}, u32[]{:S(2)}) collective-permute-start(f32[432,1280]{1,0:T(8,128)} %constant_dynamic-slice_fusion.6), channel_id=1, source_target_pairs={{0,16},{8,24},{16,0},{24,8},{1,17},{9,25},{17,1},{25,9},{2,18},{10... | collective-permute-start | bytes 6635528 | tf_op jit(solution)/shard_map/ppermute | solution.py:212
  14.4 144.4 %collective-permute-start.2 = (f32[432,1280]{1,0:T(8,128)S(1)}, f32[432,1280]{1,0:T(8,128)}, u32[]{:S(2)}, u32[]{:S(2)}) collective-permute-start(f32[432,1280]{1,0:T(8,128)S(1)} %constant_dynamic-slice_fusion.7), channel_id=1, source_target_pairs={{0,24},{8,16},{16,8},{24,0},{1,25},{9,17},{17,9},{25,1},{2,26},{10... | collective-permute-start | bytes 6635528 | tf_op jit(solution)/shard_map/ppermute | solution.py:212
  178.4 14.6 %collective-permute-start.3 = (f32[24,256,256]{2,1,0:T(8,128)}, f32[24,256,256]{2,1,0:T(8,128)}, u32[]{:S(2)}, u32[]{:S(2)}) collective-permute-start(f32[24,256,256]{2,1,0:T(8,128)} %get-tuple-element.104), channel_id=1, source_target_pairs={{0,2},{2,0},{4,6},{6,4},{1,3},{3,1},{5,7},{7,5},{8,10},{10,8},{12,... | collective-permute-start | bytes 18874376 | tf_op jit(solution)/shard_map/ppermute | solution.py:212
  199.9 49.6 %collective-permute-start.4 = (f32[1024,256]{1,0:T(8,128)}, f32[1024,256]{1,0:T(8,128)}, u32[]{:S(2)}, u32[]{:S(2)}) collective-permute-start(f32[1024,256]{1,0:T(8,128)} %get-tuple-element.105), channel_id=1, source_target_pairs={{0,4},{2,6},{4,0},{6,2},{1,5},{3,7},{5,1},{7,3},{8,12},{10,14},{12... | collective-permute-start | bytes 3145736 | tf_op jit(solution)/shard_map/ppermute | solution.py:212
  201.4 48.1 %collective-permute-start.5 = (f32[1024,256]{1,0:T(8,128)}, f32[1024,256]{1,0:T(8,128)}, u32[]{:S(2)}, u32[]{:S(2)}) collective-permute-start(f32[1024,256]{1,0:T(8,128)} %get-tuple-element.106), channel_id=1, source_target_pairs={{0,1},{1,0},{2,3},{3,2},{4,5},{5,4},{6,7},{7,6},{8,9},{9,8},{10,11... | collective-permute-start | bytes 3145736 | tf_op jit(solution)/shard_map/ppermute | solution.py:212
  202.9 70.1 %collective-permute-start.6 = (f32[1024,256]{1,0:T(8,128)}, f32[1024,256]{1,0:T(8,128)}, u32[]{:S(2)}, u32[]{:S(2)}) collective-permute-start(f32[1024,256]{1,0:T(8,128)} %get-tuple-element.107), channel_id=1, source_target_pairs={{0,8},{8,0},{16,24},{24,16},{1,9},{9,1},{17,25},{25,17},{2,10},{10... | collective-permute-start | bytes 3145736 | tf_op jit(solution)/shard_map/ppermute | solution.py:212
  275.4 19.3 %copy-start.7 = (f32[512,256]{1,0:T(8,128)S(1)}, f32[512,256]{1,0:T(8,128)}, u32[]{:S(2)}) copy-start(f32[512,256]{1,0:T(8,128)} %get-tuple-element.174) | copy-start | bytes 1572868
  279.7 13.4 %collective-permute-start.7 = (f32[512,256]{1,0:T(8,128)}, f32[512,256]{1,0:T(8,128)S(1)}, u32[]{:S(2)}, u32[]{:S(2)}) collective-permute-start(f32[512,256]{1,0:T(8,128)} %get-tuple-element.111), channel_id=1, source_target_pairs={{0,1},{1,0},{2,3},{3,2},{4,5},{5,4},{6,7},{7,6},{8,9},{9,8},{10,11... | collective-permute-start | bytes 1572872 | tf_op jit(solution)/shard_map/ppermute | solution.py:212
  280.2 13.1 %collective-permute-start.8 = (f32[512,256]{1,0:T(8,128)}, f32[512,256]{1,0:T(8,128)S(1)}, u32[]{:S(2)}, u32[]{:S(2)}) collective-permute-start(f32[512,256]{1,0:T(8,128)} %get-tuple-element.112), channel_id=1, source_target_pairs={{0,8},{8,0},{16,24},{24,16},{1,9},{9,1},{17,25},{25,17},{2,10},{10... | collective-permute-start | bytes 1572872 | tf_op jit(solution)/shard_map/ppermute | solution.py:212
  281.9 12.7 %collective-permute-start.9 = (f32[512,256]{1,0:T(8,128)}, f32[512,256]{1,0:T(8,128)}, u32[]{:S(2)}, u32[]{:S(2)}) collective-permute-start(f32[512,256]{1,0:T(8,128)} %get-tuple-element.113), channel_id=1, source_target_pairs={{0,4},{2,6},{4,0},{6,2},{1,5},{3,7},{5,1},{7,3},{8,12},{10,14},{12... | collective-permute-start | bytes 1572872 | tf_op jit(solution)/shard_map/ppermute | solution.py:212
  293.0 1.6 copy-start.12
  297.6 6.4 %collective-permute-start.10 = (f32[256,256]{1,0:T(8,128)S(1)}, f32[256,256]{1,0:T(8,128)S(1)}, u32[]{:S(2)}, u32[]{:S(2)}) collective-permute-start(f32[256,256]{1,0:T(8,128)S(1)} %get-tuple-element.117), channel_id=1, source_target_pairs={{0,8},{8,0},{16,24},{24,16},{1,9},{9,1},{17,25},{25,17},{2,10},{10... | collective-permute-start | bytes 786440 | tf_op jit(solution)/shard_map/ppermute | solution.py:212
  298.3 6.6 %collective-permute-start.11 = (f32[256,256]{1,0:T(8,128)}, f32[256,256]{1,0:T(8,128)S(1)}, u32[]{:S(2)}, u32[]{:S(2)}) collective-permute-start(f32[256,256]{1,0:T(8,128)} %get-tuple-element.118), channel_id=1, source_target_pairs={{0,4},{2,6},{4,0},{6,2},{1,5},{3,7},{5,1},{7,3},{8,12},{10,14},{12... | collective-permute-start | bytes 786440 | tf_op jit(solution)/shard_map/ppermute | solution.py:212
  298.8 6.4 %collective-permute-start.12 = (f32[256,256]{1,0:T(8,128)S(1)}, f32[256,256]{1,0:T(8,128)S(1)}, u32[]{:S(2)}, u32[]{:S(2)}) collective-permute-start(f32[256,256]{1,0:T(8,128)S(1)} %get-tuple-element.119), channel_id=1, source_target_pairs={{0,1},{1,0},{2,3},{3,2},{4,5},{5,4},{6,7},{7,6},{8,9},{9,8},{10,11... | collective-permute-start | bytes 786440 | tf_op jit(solution)/shard_map/ppermute | solution.py:212
  305.3 12.4 %collective-permute-start.13 = (f32[128,256]{1,0:T(8,128)S(1)}, f32[128,256]{1,0:T(8,128)S(1)}, u32[]{:S(2)}, u32[]{:S(2)}) collective-permute-start(f32[128,256]{1,0:T(8,128)S(1)} %dynamic-slice_add_fusion.20), channel_id=1, source_target_pairs={{0,16},{8,24},{16,0},{24,8},{1,17},{9,25},{17,1},{25,9},{2,18},{10... | collective-permute-start | bytes 393224 | tf_op jit(solution)/shard_map/ppermute | solution.py:212
  307.7 12.8 %collective-permute-start.14 = (f32[128,256]{1,0:T(8,128)S(1)}, f32[128,256]{1,0:T(8,128)S(1)}, u32[]{:S(2)}, u32[]{:S(2)}) collective-permute-start(f32[128,256]{1,0:T(8,128)S(1)} %dynamic-slice_add_fusion.19), channel_id=1, source_target_pairs={{0,16},{8,24},{16,0},{24,8},{1,17},{9,25},{17,1},{25,9},{2,18},{10... | collective-permute-start | bytes 393224 | tf_op jit(solution)/shard_map/ppermute | solution.py:212
  308.3 14.3 %collective-permute-start.15 = (f32[128,256]{1,0:T(8,128)S(1)}, f32[128,256]{1,0:T(8,128)S(1)}, u32[]{:S(2)}, u32[]{:S(2)}) collective-permute-start(f32[128,256]{1,0:T(8,128)S(1)} %dynamic-slice_add_fusion.18), channel_id=1, source_target_pairs={{0,16},{8,24},{16,0},{24,8},{1,17},{9,25},{17,1},{25,9},{2,18},{10... | collective-permute-start | bytes 393224 | tf_op jit(solution)/shard_map/ppermute | solution.py:212
  322.7 14.4 %collective-permute-start.16 = (f32[128,256]{1,0:T(8,128)S(1)}, f32[128,256]{1,0:T(8,128)S(1)}, u32[]{:S(2)}, u32[]{:S(2)}) collective-permute-start(f32[128,256]{1,0:T(8,128)S(1)} %add_add_fusion.2), channel_id=1, source_target_pairs={{0,16},{8,24},{16,0},{24,8},{1,17},{9,25},{17,1},{25,9},{2,18},{10... | collective-permute-start | bytes 393224 | tf_op jit(solution)/shard_map/ppermute | solution.py:212
  322.8 17.1 %collective-permute-start.17 = (f32[128,256]{1,0:T(8,128)S(1)}, f32[128,256]{1,0:T(8,128)S(1)}, u32[]{:S(2)}, u32[]{:S(2)}) collective-permute-start(f32[128,256]{1,0:T(8,128)S(1)} %add_add_fusion.1), channel_id=1, source_target_pairs={{0,16},{8,24},{16,0},{24,8},{1,17},{9,25},{17,1},{25,9},{2,18},{10... | collective-permute-start | bytes 393224 | tf_op jit(solution)/shard_map/ppermute | solution.py:212
  325.8 16.7 %collective-permute-start.18 = (f32[128,256]{1,0:T(8,128)S(1)}, f32[128,256]{1,0:T(8,128)S(1)}, u32[]{:S(2)}, u32[]{:S(2)}) collective-permute-start(f32[128,256]{1,0:T(8,128)S(1)} %add_add_fusion), channel_id=1, source_target_pairs={{0,16},{8,24},{16,0},{24,8},{1,17},{9,25},{17,1},{25,9},{2,18},{10... | collective-permute-start | bytes 393224 | tf_op jit(solution)/shard_map/ppermute | solution.py:212
  342.5 8.2 %collective-permute-start.19 = (f32[256,256]{1,0:T(8,128)S(1)}, f32[256,256]{1,0:T(8,128)S(1)}, u32[]{:S(2)}, u32[]{:S(2)}) collective-permute-start(f32[256,256]{1,0:T(8,128)S(1)} %constant_dynamic-update-slice_fusion.5), channel_id=1, source_target_pairs={{0,8},{8,0},{16,24},{24,16},{1,9},{9,1},{17,25},{25,17},{2,10},{10... | collective-permute-start | bytes 786440 | tf_op jit(solution)/shard_map/ppermute | solution.py:212
  342.6 8.2 %collective-permute-start.20 = (f32[256,256]{1,0:T(8,128)S(1)}, f32[256,256]{1,0:T(8,128)S(1)}, u32[]{:S(2)}, u32[]{:S(2)}) collective-permute-start(f32[256,256]{1,0:T(8,128)S(1)} %constant_dynamic-update-slice_fusion.2), channel_id=1, source_target_pairs={{0,4},{2,6},{4,0},{6,2},{1,5},{3,7},{5,1},{7,3},{8,12},{10,14},{12... | collective-permute-start | bytes 786440 | tf_op jit(solution)/shard_map/ppermute | solution.py:212
  344.2 7.8 %collective-permute-start.21 = (f32[256,256]{1,0:T(8,128)S(1)}, f32[256,256]{1,0:T(8,128)S(1)}, u32[]{:S(2)}, u32[]{:S(2)}) collective-permute-start(f32[256,256]{1,0:T(8,128)S(1)} %constant_dynamic-update-slice_fusion), channel_id=1, source_target_pairs={{0,1},{1,0},{2,3},{3,2},{4,5},{5,4},{6,7},{7,6},{8,9},{9,8},{10,11... | collective-permute-start | bytes 786440 | tf_op jit(solution)/shard_map/ppermute | solution.py:212
  352.1 12.7 %collective-permute-start.22 = (f32[512,256]{1,0:T(8,128)S(1)}, f32[512,256]{1,0:T(8,128)S(1)}, u32[]{:S(2)}, u32[]{:S(2)}) collective-permute-start(f32[512,256]{1,0:T(8,128)S(1)} %pad_maximum_fusion.3), channel_id=1, source_target_pairs={{0,1},{1,0},{2,3},{3,2},{4,5},{5,4},{6,7},{7,6},{8,9},{9,8},{10,11... | collective-permute-start | bytes 1572872 | tf_op jit(solution)/shard_map/ppermute | solution.py:212
  353.0 12.4 %collective-permute-start.23 = (f32[512,256]{1,0:T(8,128)S(1)}, f32[512,256]{1,0:T(8,128)S(1)}, u32[]{:S(2)}, u32[]{:S(2)}) collective-permute-start(f32[512,256]{1,0:T(8,128)S(1)} %pad_maximum_fusion.4), channel_id=1, source_target_pairs={{0,8},{8,0},{16,24},{24,16},{1,9},{9,1},{17,25},{25,17},{2,10},{10... | collective-permute-start | bytes 1572872 | tf_op jit(solution)/shard_map/ppermute | solution.py:212
  354.7 11.9 %collective-permute-start.24 = (f32[512,256]{1,0:T(8,128)S(1)}, f32[512,256]{1,0:T(8,128)S(1)}, u32[]{:S(2)}, u32[]{:S(2)}) collective-permute-start(f32[512,256]{1,0:T(8,128)S(1)} %pad_maximum_fusion.5), channel_id=1, source_target_pairs={{0,4},{2,6},{4,0},{6,2},{1,5},{3,7},{5,1},{7,3},{8,12},{10,14},{12... | collective-permute-start | bytes 1572872 | tf_op jit(solution)/shard_map/ppermute | solution.py:212
  366.8 22.3 %collective-permute-start.25 = (f32[1024,256]{1,0:T(8,128)S(1)}, f32[1024,256]{1,0:T(8,128)S(1)}, u32[]{:S(2)}, u32[]{:S(2)}) collective-permute-start(f32[1024,256]{1,0:T(8,128)S(1)} %pad_maximum_fusion), channel_id=1, source_target_pairs={{0,4},{2,6},{4,0},{6,2},{1,5},{3,7},{5,1},{7,3},{8,12},{10,14},{12... | collective-permute-start | bytes 3145736 | tf_op jit(solution)/shard_map/ppermute | solution.py:212
  367.4 22.0 %collective-permute-start.26 = (f32[1024,256]{1,0:T(8,128)S(1)}, f32[1024,256]{1,0:T(8,128)S(1)}, u32[]{:S(2)}, u32[]{:S(2)}) collective-permute-start(f32[1024,256]{1,0:T(8,128)S(1)} %pad_maximum_fusion.1), channel_id=1, source_target_pairs={{0,1},{1,0},{2,3},{3,2},{4,5},{5,4},{6,7},{7,6},{8,9},{9,8},{10,11... | collective-permute-start | bytes 3145736 | tf_op jit(solution)/shard_map/ppermute | solution.py:212
  368.5 21.6 %collective-permute-start.27 = (f32[1024,256]{1,0:T(8,128)S(1)}, f32[1024,256]{1,0:T(8,128)S(1)}, u32[]{:S(2)}, u32[]{:S(2)}) collective-permute-start(f32[1024,256]{1,0:T(8,128)S(1)} %pad_maximum_fusion.2), channel_id=1, source_target_pairs={{0,8},{8,0},{16,24},{24,16},{1,9},{9,1},{17,25},{25,17},{2,10},{10... | collective-permute-start | bytes 3145736 | tf_op jit(solution)/shard_map/ppermute | solution.py:212
  369.4 20.8 %copy-start.1 = (f32[3072,256]{1,0:T(8,128)}, f32[3072,256]{1,0:T(8,128)S(1)}, u32[]{:S(2)}) copy-start(f32[3072,256]{1,0:T(8,128)S(1)} %constant_dynamic-update-slice_fusion.6) | copy-start | bytes 9437188
  369.4 22.7 %copy-start.11 = (f32[144,1280]{1,0:T(8,128)S(1)}, f32[144,1280]{1,0:T(8,128)}, u32[]{:S(2)}) copy-start(f32[144,1280]{1,0:T(8,128)} %constant_dynamic-slice_fusion.2) | copy-start | bytes 2211844
  369.4 23.6 %collective-permute-start.28 = (f32[3072,256]{1,0:T(8,128)S(1)}, f32[3072,256]{1,0:T(8,128)S(1)}, u32[]{:S(2)}, u32[]{:S(2)}) collective-permute-start(f32[3072,256]{1,0:T(8,128)S(1)} %constant_dynamic-update-slice_fusion.6), channel_id=1, source_target_pairs={{0,2},{2,0},{4,6},{6,4},{1,3},{3,1},{5,7},{7,5},{8,10},{10,8},{12,... | collective-permute-start | bytes 9437192 | tf_op jit(solution)/shard_map/ppermute | solution.py:212
  390.2 7.5 %copy-start = (f32[3072,256]{1,0:T(8,128)}, f32[3072,256]{1,0:T(8,128)S(1)}, u32[]{:S(2)}) copy-start(f32[3072,256]{1,0:T(8,128)S(1)} %constant_dynamic-update-slice_fusion.9) | copy-start | bytes 9437188
  390.2 5.7 collective-permute-start.29
  392.0 58.2 %collective-permute-start.30 = (f32[144,1280]{1,0:T(8,128)S(1)}, f32[144,1280]{1,0:T(8,128)S(1)}, u32[]{:S(2)}, u32[]{:S(2)}) collective-permute-start(f32[144,1280]{1,0:T(8,128)S(1)} %copy-done.11), channel_id=1, source_target_pairs={{0,8},{8,0},{16,24},{24,16},{1,9},{9,1},{17,25},{25,17},{2,10},{10... | collective-permute-start | bytes 2211848 | tf_op jit(solution)/shard_map/ppermute | solution.py:212
  393.0 2.9 copy-start.2
  395.9 1.7 copy-start.3
  397.7 19.7 %copy-start.10 = (f32[144,1280]{1,0:T(8,128)S(1)}, f32[144,1280]{1,0:T(8,128)}, u32[]{:S(2)}) copy-start(f32[144,1280]{1,0:T(8,128)} %constant_dynamic-slice_fusion.1) | copy-start | bytes 2211844
  415.1 199.4 %collective-permute-start.34 = (f32[432,1280]{1,0:T(8,128)}, f32[432,1280]{1,0:T(8,128)}, u32[]{:S(2)}, u32[]{:S(2)}) collective-permute-start(f32[432,1280]{1,0:T(8,128)} %correction.7), channel_id=1, source_target_pairs={{0,8},{8,0},{16,24},{24,16},{1,9},{9,1},{17,25},{25,17},{2,10},{10... | collective-permute-start | bytes 6635528 | tf_op jit(solution)/shard_map/ppermute | solution.py:212
  417.4 64.5 %collective-permute-start.31 = (f32[144,1280]{1,0:T(8,128)S(1)}, f32[144,1280]{1,0:T(8,128)S(1)}, u32[]{:S(2)}, u32[]{:S(2)}) collective-permute-start(f32[144,1280]{1,0:T(8,128)S(1)} %copy-done.10), channel_id=1, source_target_pairs={{0,16},{8,24},{16,0},{24,8},{1,17},{9,25},{17,1},{25,9},{2,18},{10... | collective-permute-start | bytes 2211848 | tf_op jit(solution)/shard_map/ppermute | solution.py:212
  417.4 80.8 %collective-permute-start.32 = (f32[144,1280]{1,0:T(8,128)}, f32[144,1280]{1,0:T(8,128)S(1)}, u32[]{:S(2)}, u32[]{:S(2)}) collective-permute-start(f32[144,1280]{1,0:T(8,128)} %constant_dynamic-slice_fusion), channel_id=1, source_target_pairs={{0,24},{8,16},{16,8},{24,0},{1,25},{9,17},{17,9},{25,1},{2,26},{10... | collective-permute-start | bytes 2211848 | tf_op jit(solution)/shard_map/ppermute | solution.py:212
  434.3 118.9 %collective-permute-start.36 = (f32[288,1280]{1,0:T(8,128)}, f32[288,1280]{1,0:T(8,128)S(1)}, u32[]{:S(2)}, u32[]{:S(2)}) collective-permute-start(f32[288,1280]{1,0:T(8,128)} %correction.9), channel_id=1, source_target_pairs={{0,24},{8,16},{16,8},{24,0},{1,25},{9,17},{17,9},{25,1},{2,26},{10... | collective-permute-start | bytes 4423688 | tf_op jit(solution)/shard_map/ppermute | solution.py:212
  450.3 47.9 %copy-start.4 = (f32[144,1280]{1,0:T(8,128)}, f32[144,1280]{1,0:T(8,128)S(1)}, u32[]{:S(2)}) copy-start(f32[144,1280]{1,0:T(8,128)S(1)} %collective-permute-done.30.refs_5_) | copy-start | bytes 2211844
  450.3 160.1 %collective-permute-start.35 = (f32[288,1280]{1,0:T(8,128)}, f32[288,1280]{1,0:T(8,128)S(1)}, u32[]{:S(2)}, u32[]{:S(2)}) collective-permute-start(f32[288,1280]{1,0:T(8,128)} %correction.8), channel_id=1, source_target_pairs={{0,16},{8,24},{16,0},{24,8},{1,17},{9,25},{17,1},{25,9},{2,18},{10... | collective-permute-start | bytes 4423688 | tf_op jit(solution)/shard_map/ppermute | solution.py:212
  481.9 16.2 %copy-start.5 = (f32[144,1280]{1,0:T(8,128)}, f32[144,1280]{1,0:T(8,128)S(1)}, u32[]{:S(2)}) copy-start(f32[144,1280]{1,0:T(8,128)S(1)} %collective-permute-done.31.refs_6_) | copy-start | bytes 2211844
  512.5 107.2 %collective-permute-start.33 = (f32[144,1280]{1,0:T(8,128)}, f32[144,1280]{1,0:T(8,128)}, u32[]{:S(2)}, u32[]{:S(2)}) collective-permute-start(f32[144,1280]{1,0:T(8,128)} %correction.6), channel_id=1, source_target_pairs={{0,8},{8,0},{16,24},{24,16},{1,9},{9,1},{17,25},{25,17},{2,10},{10... | collective-permute-start | bytes 2211848 | tf_op jit(solution)/shard_map/ppermute | solution.py:212
  (3 other events, 3.1 us)

commit v3 on v2

--- a/solution.py
+++ b/solution.py
@@ -31,12 +31,10 @@
 
 def load_kernel(n, per, *refs):
     pieces = refs[:n]
-    high, low, turned_high, turned_low = refs[n:]
+    high, low = refs[n:]
     for d in range(n):
         for s in range(per):
-            x = pieces[d][:, s * PANEL : (s + 1) * PANEL]
-            high[d * per + s], low[d * per + s] = split(x)
-            turned_high[d * per + s], turned_low[d * per + s] = split(x.T)
+            high[d * per + s], low[d * per + s] = split(pieces[d][:, s * PANEL : (s + 1) * PANEL])
 
 
 def gram_first_kernel(scale, n, per, where, *refs):
@@ -50,11 +48,11 @@
     gram_kernel(scale, where, *kept, gram)
 
 
-def gram_kernel(scale, where, high, low, turned_high, turned_low, gram):
+def gram_kernel(scale, where, high, low, gram):
     for t in range(GROUP):
         k = pl.program_id(0) * GROUP + t
         i, j = where[k, 0], where[k, 1]
-        gram[t] = scale * product((turned_high[i], turned_low[i]), (high[j], low[j]), ((1,), (0,)))
+        gram[t] = scale * product((high[i], low[i]), (high[j], low[j]), ((0,), (0,)))
 
 
 def still(shape):
@@ -69,7 +67,7 @@
         slots = n * width // PANEL
     else:
         slots, rows, _ = arrays[0].shape
-    kept = [(slots, rows, PANEL)] * 2 + [(slots, PANEL, rows)] * 2
+    kept = [(slots, rows, PANEL)] * 2
     gram_spec = pl.BlockSpec((GROUP, PANEL, PANEL), lambda k, w: (k, 0, 0))
     gram_shape = jax.ShapeDtypeStruct((count, PANEL, PANEL), jnp.float32)
     return pl.pallas_call(
@@ -201,6 +199,91 @@
         cost_estimate=pl.CostEstimate(flops=3 * size * width, bytes_accessed=16 * size * width, transcendentals=0),
         name="place",
     )(at[None] // block, part, weight, *earlier)
+
+
+def eager_kernel(parts, per, table, *refs):
+    grams = refs[:parts]
+    high, low, out, held, high_here, low_here, gram_sem, side_sem = refs[parts:]
+    slots, rows, _ = high_here.shape
+    size = grams[0].shape[0]
+
+    def sides(g):
+        part = pl.ds(g * per, per)
+        return [
+            pltpu.make_async_copy(far.at[part, pl.ds(0, rows)], near.at[part], side_sem.at[which, g])
+            for which, (far, near) in enumerate(((high, high_here), (low, low_here)))
+        ]
+
+    for g in range(slots // per):
+        for copy in sides(g):
+            copy.start()
+
+    def each(do):
+        for part in range(parts):
+
+            def one(t, carry):
+                k = part * size + t
+                first, second = table[k, 2], table[k, 3]
+
+                @pl.when(jnp.maximum(first, second) >= 0)
+                def _():
+                    do(k, pltpu.make_async_copy(grams[part].at[t], held.at[k], gram_sem.at[k]))
+
+                return carry
+
+            lax.fori_loop(0, size, one, 0)
+
+    each(lambda k, copy: copy.start())
+    out[...] = jnp.zeros_like(out)
+    for g in range(slots // per):
+        for copy in sides(g):
+            copy.wait()
+
+    def add(k, copy):
+        copy.wait()
+        i, j, first, second = table[k, 0], table[k, 1], table[k, 2], table[k, 3]
+
+        @pl.when(first >= 0)
+        def _():
+            at = pl.ds(pl.multiple_of(first * PANEL, PANEL), PANEL)
+            out[:, at] += product((high_here[j], low_here[j]), split(held[k]), ((1,), (1,)))
+
+        @pl.when(second >= 0)
+        def _():
+            at = pl.ds(pl.multiple_of(second * PANEL, PANEL), PANEL)
+            out[:, at] += product((high_here[i], low_here[i]), split(held[k]), ((1,), (0,)))
+
+    each(add)
+
+
+def eager_call(table, grams, arrays, rows, per):
+    slots, count = arrays[0].shape[0], table.shape[0]
+    return pl.pallas_call(
+        functools.partial(eager_kernel, len(grams), per),
+        grid_spec=pltpu.PrefetchScalarGridSpec(
+            num_scalar_prefetch=1,
+            grid=(1,),
+            in_specs=[pl.BlockSpec(memory_space=pl.ANY)] * (len(grams) + 2),
+            out_specs=still((rows, per * PANEL)),
+            scratch_shapes=[
+                pltpu.VMEM((count, PANEL, PANEL), jnp.float32),
+                pltpu.VMEM((slots, rows, PANEL), jnp.bfloat16),
+                pltpu.VMEM((slots, rows, PANEL), jnp.bfloat16),
+                pltpu.SemaphoreType.DMA((count,)),
+                pltpu.SemaphoreType.DMA((2, slots // per)),
+            ],
+        ),
+        out_shape=jax.ShapeDtypeStruct((rows, per * PANEL), jnp.float32),
+        compiler_params=pltpu.CompilerParams(
+            dimension_semantics=("arbitrary",), vmem_limit_bytes=VMEM_LIMIT
+        ),
+        cost_estimate=pl.CostEstimate(
+            flops=3 * count * PANEL * PANEL * rows,
+            bytes_accessed=4 * slots * rows * PANEL + 4 * count * PANEL * PANEL,
+            transcendentals=0,
+        ),
+        name="eager",
+    )(table, *grams, *arrays)
 
 
 together = lax.optimization_barrier
@@ -338,15 +421,14 @@
     there_other = flip(there, core_dim)
     grams = [g.reshape(count // 4, PANEL, PANEL) for g in (here, there, here_other, there_other)]
 
-    ready = []
+    ready = [[], [], [], []]
     for d in range(n - 1, -1, -1):
-        found = [((z ^ d) * rows, correction_call(tables[d], grams, panels[:2], less if d >= top else rows, per))]
+        found = [((z ^ d) * rows, eager_call(tables[d], grams, panels, less if d >= top else rows, per))]
         if more and d < top:
             found.append(((z ^ d ^ top) * rows + less, correction_call(tables[d], grams, mirrored, more, per)))
-        if d:
-            ready += [(at, flip(part, ("tri", d))) for at, part in found]
-        else:
-            ready = found + ready
+        when = 0 if d == 0 else 1 if d > top else 3 if d == top else 2
+        ready[when] += [(at, flip(part, ("tri", d)) if d else part) for at, part in found]
+    ready = sum(ready, [])
 
     block = math.gcd(rows, more)
     placed = ()

time: 624 us -> 611 us (0.979)
  Pallas kernels: 147 us -> 135 us
    pallas_call x6 -> x2, Pallas kernels: 91.6 us -> 27.7 us  [correction_call(): pl.pallas_call(functools.partial(correction_kernel, len(grams), len(array...]
    pallas_call x0 -> x4, Pallas kernels: none -> 58.2 us  [eager_call(): pl.pallas_call(functools.partial(eager_kernel, len(grams), per), grid_spe...]
    pallas_call x2, Pallas kernels: 34.2 us -> 27.4 us  [gram_call(): pl.pallas_call(functools.partial(gram_first_kernel, scale, n, slots // n)...]
  transfers between devices with their start and end apart: 37 -> 37, of which waited for: 28 -> 26; matrix products, arithmetic and copies ran while one was open for 2% -> 3% of each run, Pallas kernels for 20% -> 17%
where the time goes in v3:
time: 611 us; the launch traced here: 610 us
  waiting for transfers between devices  340 us (56%)
  Pallas kernels  135 us (22%)
  starting transfers between devices  87.7 us (14%)
  local copies, waits for them, and re-layouts  26.6 us (4%)
  other arithmetic  19.9 us (3%)
    ppermute x37, waiting for transfers between devices, flip(): return lax.ppermute(value, axis, pairs)  340 us
    ppermute x37, starting transfers between devices, flip(): return lax.ppermute(value, axis, pairs)  87.7 us
    pallas_call x4, Pallas kernels, eager_call(): pl.pallas_call(functools.partial(eager_kernel, len(grams), per), grid_spe...  58.2 us
    pallas_call x2, Pallas kernels, correction_call(): pl.pallas_call(functools.partial(correction_kernel, len(grams), len(array...  27.7 us
    pallas_call x2, Pallas kernels, gram_call(): pl.pallas_call(functools.partial(gram_first_kernel, scale, n, slots // n)...  27.4 us
    pallas_call x6, Pallas kernels, place_call(): pl.pallas_call(place_kernel, grid_spec=pltpu.PrefetchScalarGridSpec(num_s...  21.4 us
    add x10, other arithmetic, cut(): sum((lax.dynamic_slice_in_dim(t, base + start, rows, 0) for base, t in te...  16.6 us
  transfers between devices with their start and end apart: 37, of which 26 were waited for; matrix products, arithmetic and copies ran while one was open for 3% of the time, Pallas kernels for 17%

profile of v3, /device:TPU:0, one launch (start us, length us, event | category | flops | bytes accessed | tf_op | source)
XLA Modules:
  0.0 609.9 jit_solution(10031567693627918423)
XLA Ops:
  2.4 3.2 constant_dynamic-slice_fusion.6
  5.6 3.1 constant_dynamic-slice_fusion.5
  8.7 3.1 collective-permute-start
  11.8 2.6 collective-permute-start.1
  14.5 2.0 constant_dynamic-slice_fusion.3.refs_4_
  20.6 2.0 constant_dynamic-slice_fusion
  24.3 3.1 constant_dynamic-slice_fusion.4.refs_0_
  27.4 79.5 %collective-permute-done.refs_1_ = f32[432,1280]{1,0:T(8,128)} collective-permute-done((f32[432,1280]{1,0:T(8,128)}, f32[432,1280]{1,0:T(8,128)}, u32[]{:S(2)}, u32[]{:S(2)}) %collective-permute-start) | collective-permute-done | bytes 2211872 | tf_op jit(solution)/shard_map/ppermute | solution.py:295
  106.8 51.9 %collective-permute-done.1.refs_2_ = f32[432,1280]{1,0:T(8,128)} collective-permute-done((f32[432,1280]{1,0:T(8,128)}, f32[432,1280]{1,0:T(8,128)}, u32[]{:S(2)}, u32[]{:S(2)}) %collective-permute-start.1) | collective-permute-done | bytes 2211872 | tf_op jit(solution)/shard_map/ppermute | solution.py:295
  158.8 15.6 %gram_first.1 = (f32[24,256,256]{2,1,0:T(8,128)}, bf16[20,432,256]{2,1,0:T(8,128)(2,1)}, bf16[20,432,256]{2,1,0:T(8,128)(2,1)}) custom-call(s32[24,2]{1,0:T(8,128)} %get-tuple-element.183.where, f32[432,1280]{1,0:T(8,128)} %constant_dynamic-slice_fusion.4.refs_0_, f32[432,1280]{1,0:T(8,128)} %collective-permute-done.refs_1_, ...), custom_call_target="tpu_custom_call" | custom-call | flops 4076863488 | bytes 23986176 | tf_op jit(solution)/shard_map/gram_first/pallas_call | solution.py:73
  174.3 11.9 %gram.1 = f32[24,256,256]{2,1,0:T(8,128)} custom-call(s32[24,2]{1,0:T(8,128)} %get-tuple-element.182.where, bf16[20,432,256]{2,1,0:T(8,128)(2,1)} %get-tuple-element.98.high.refs_4_, bf16[20,432,256]{2,1,0:T(8,128)(2,1)} %get-tuple-element.99.low.refs_5_), custom_call_target="tpu_custom_call" | custom-call | flops 4076863488 | bytes 23986176 | tf_op jit(solution)/shard_map/gram/pallas_call | solution.py:73
  186.2 6.9 %dynamic-slice_add_fusion = (f32[1024,256]{1,0:T(8,128)S(1)}, f32[1024,256]{1,0:T(8,128)S(1)}, f32[1024,256]{1,0:T(8,128)}, f32[1024,256]{1,0:T(8,128)}, f32[1024,256]{1,0:T(8,128)}, /*index=5*/f32[1024,256]{1,0:T(8,128)S(1)}) fusion(f32[6144,256]{1,0:T(8,128)} %bitcast.3, s32[]{:T(128)S(6)} %select_n.589, f32[6144,256]{1,0:T(8,128)} %bitcast.42, ...), kind=kLoop, calls=%fused_computation.4 | loop fusion | flops 1572864 | bytes 18874392 | tf_op jit(solution)/shard_map/add | solution.py:312
  196.1 46.6 %collective-permute-start.6 = (f32[1024,256]{1,0:T(8,128)}, f32[1024,256]{1,0:T(8,128)}, u32[]{:S(2)}, u32[]{:S(2)}) collective-permute-start(f32[1024,256]{1,0:T(8,128)} %get-tuple-element.103), channel_id=1, source_target_pairs={{0,8},{8,0},{16,24},{24,16},{1,9},{9,1},{17,25},{25,17},{2,10},{10... | collective-permute-start | bytes 3145736 | tf_op jit(solution)/shard_map/ppermute | solution.py:295
  242.7 23.6 %collective-permute-done.6 = f32[1024,256]{1,0:T(8,128)} collective-permute-done((f32[1024,256]{1,0:T(8,128)}, f32[1024,256]{1,0:T(8,128)}, u32[]{:S(2)}, u32[]{:S(2)}) %collective-permute-start.6) | collective-permute-done | bytes 1048608 | tf_op jit(solution)/shard_map/ppermute | solution.py:295
  266.3 2.4 dynamic-slice_add_fusion.6
  268.7 2.2 dynamic-slice_add_fusion.11
  270.9 2.1 dynamic-slice_add_fusion.7
  275.8 10.6 %collective-permute-done.7 = f32[512,256]{1,0:T(8,128)S(1)} collective-permute-done((f32[512,256]{1,0:T(8,128)}, f32[512,256]{1,0:T(8,128)S(1)}, u32[]{:S(2)}, u32[]{:S(2)}) %collective-permute-start.7) | collective-permute-done | bytes 524320 | tf_op jit(solution)/shard_map/ppermute | solution.py:295
  293.5 3.8 collective-permute-done.10
  298.6 2.4 collective-permute-start.13
  301.6 2.3 collective-permute-start.15
  303.9 7.1 %collective-permute-done.13 = f32[128,256]{1,0:T(8,128)S(1)} collective-permute-done((f32[128,256]{1,0:T(8,128)S(1)}, f32[128,256]{1,0:T(8,128)S(1)}, u32[]{:S(2)}, u32[]{:S(2)}) %collective-permute-start.13) | collective-permute-done | bytes 131104 | tf_op jit(solution)/shard_map/ppermute | solution.py:295
  311.0 2.8 collective-permute-done.14
  313.8 2.2 collective-permute-done.15
  316.2 3.0 collective-permute-start.17
  319.3 11.0 %collective-permute-done.16 = f32[128,256]{1,0:T(8,128)S(1)} collective-permute-done((f32[128,256]{1,0:T(8,128)S(1)}, f32[128,256]{1,0:T(8,128)S(1)}, u32[]{:S(2)}, u32[]{:S(2)}) %collective-permute-start.16) | collective-permute-done | bytes 131104 | tf_op jit(solution)/shard_map/ppermute | solution.py:295
  330.4 2.8 collective-permute-done.17
  333.2 2.7 collective-permute-done.18
  338.2 6.0 collective-permute-done.19
  348.6 9.9 %collective-permute-done.22 = f32[512,256]{1,0:T(8,128)S(1)} collective-permute-done((f32[512,256]{1,0:T(8,128)S(1)}, f32[512,256]{1,0:T(8,128)S(1)}, u32[]{:S(2)}, u32[]{:S(2)}) %collective-permute-start.22) | collective-permute-done | bytes 524320 | tf_op jit(solution)/shard_map/ppermute | solution.py:295
  363.1 19.3 %collective-permute-done.25 = f32[1024,256]{1,0:T(8,128)S(1)} collective-permute-done((f32[1024,256]{1,0:T(8,128)S(1)}, f32[1024,256]{1,0:T(8,128)S(1)}, u32[]{:S(2)}, u32[]{:S(2)}) %collective-permute-start.25) | collective-permute-done | bytes 1048608 | tf_op jit(solution)/shard_map/ppermute | solution.py:295
  386.0 3.8 collective-permute-done.29
  391.5 15.6 %eager.5 = f32[432,1280]{1,0:T(8,128)} custom-call(s32[48,4]{1,0:T(8,128)} %get-tuple-element.188.table, f32[12,256,256]{2,1,0:T(8,128)} %bitcast.24, f32[12,256,256]{2,1,0:T(8,128)} %bitcast.18, f32[12,256,256]{2,1,0:T(8,128)} %bitcast.30, f32[12,256,256]{2,1,0:T(8,128)} %bitcast.36, bf16[20,432,256]{2,1,0:T(8,128)(2,1)} %get-tuple-element.98.high.refs_4_, ...), custom_call_target="tpu_custom_call" | custom-call | flops 4076863488 | bytes 21430272 | tf_op jit(solution)/shard_map/eager/pallas_call | solution.py:261
  407.0 3.4 collective-permute-start.35
  410.5 4.3 collective-permute-start.33
  414.8 12.6 %eager.6 = f32[288,1280]{1,0:T(8,128)} custom-call(s32[48,4]{1,0:T(8,128)} %get-tuple-element.187.table, f32[12,256,256]{2,1,0:T(8,128)} %bitcast.25, f32[12,256,256]{2,1,0:T(8,128)} %bitcast.19, f32[12,256,256]{2,1,0:T(8,128)} %bitcast.31, f32[12,256,256]{2,1,0:T(8,128)} %bitcast.37, bf16[20,432,256]{2,1,0:T(8,128)(2,1)} %get-tuple-element.98.high.refs_4_, ...), custom_call_target="tpu_custom_call" | custom-call | flops 2717908992 | bytes 18481152 | tf_op jit(solution)/shard_map/eager/pallas_call | solution.py:261
  427.5 2.4 collective-permute-start.36
  429.9 12.2 %eager.4 = f32[288,1280]{1,0:T(8,128)} custom-call(s32[48,4]{1,0:T(8,128)} %get-tuple-element.189.table, f32[12,256,256]{2,1,0:T(8,128)} %bitcast.26, f32[12,256,256]{2,1,0:T(8,128)} %bitcast.20, f32[12,256,256]{2,1,0:T(8,128)} %bitcast.32, f32[12,256,256]{2,1,0:T(8,128)} %bitcast.38, bf16[20,432,256]{2,1,0:T(8,128)(2,1)} %get-tuple-element.98.high.refs_4_, ...), custom_call_target="tpu_custom_call" | custom-call | flops 2717908992 | bytes 18481152 | tf_op jit(solution)/shard_map/eager/pallas_call | solution.py:261
  442.1 95.9 %collective-permute-done.31.refs_5_ = f32[144,1280]{1,0:T(8,128)S(1)} collective-permute-done((f32[144,1280]{1,0:T(8,128)S(1)}, f32[144,1280]{1,0:T(8,128)S(1)}, u32[]{:S(2)}, u32[]{:S(2)}) %collective-permute-start.31) | collective-permute-done | bytes 737312 | tf_op jit(solution)/shard_map/ppermute | solution.py:295
  540.0 13.4 %correction.2 = f32[144,1280]{1,0:T(8,128)} custom-call(s32[48,4]{1,0:T(8,128)} %get-tuple-element.188.table, f32[12,256,256]{2,1,0:T(8,128)} %bitcast.27, f32[12,256,256]{2,1,0:T(8,128)} %bitcast.21, f32[12,256,256]{2,1,0:T(8,128)} %bitcast.33, f32[12,256,256]{2,1,0:T(8,128)} %bitcast.39, f32[144,1280]{1,0:T(8,128)} %constant_dynamic-slice_fusion.3.refs_4_, ...), custom_call_target="tpu_custom_call" | custom-call | flops 1358954496 | bytes 15532032 | tf_op jit(solution)/shard_map/correction/pallas_call | solution.py:155
  554.0 17.8 %eager.7.part = f32[432,1280]{1,0:T(8,128)} custom-call(s32[48,4]{1,0:T(8,128)} %get-tuple-element.160.table, f32[12,256,256]{2,1,0:T(8,128)} %bitcast.28, f32[12,256,256]{2,1,0:T(8,128)} %bitcast.22, f32[12,256,256]{2,1,0:T(8,128)} %bitcast.34, f32[12,256,256]{2,1,0:T(8,128)} %bitcast.40, bf16[20,432,256]{2,1,0:T(8,128)(2,1)} %get-tuple-element.98.high.refs_4_, ...), custom_call_target="tpu_custom_call" | custom-call | flops 4076863488 | bytes 21430272 | tf_op jit(solution)/shard_map/eager/pallas_call | solution.py:261
  571.8 5.2 place.6
  577.0 14.3 %correction.3.part = f32[144,1280]{1,0:T(8,128)} custom-call(s32[48,4]{1,0:T(8,128)} %get-tuple-element.160.table, f32[12,256,256]{2,1,0:T(8,128)} %bitcast.29, f32[12,256,256]{2,1,0:T(8,128)} %bitcast.23, f32[12,256,256]{2,1,0:T(8,128)} %bitcast.35, f32[12,256,256]{2,1,0:T(8,128)} %bitcast.41, f32[144,1280]{1,0:T(8,128)} %constant_dynamic-slice_fusion.3.refs_4_, ...), custom_call_target="tpu_custom_call" | custom-call | flops 1358954496 | bytes 15532032 | tf_op jit(solution)/shard_map/correction/pallas_call | solution.py:155
  591.3 2.5 place.7
  595.0 3.0 place.8
  598.0 5.2 place.9
  603.2 2.5 place.10
  606.8 3.0 place.11
  (119 shorter events, 44.1 us)
Async XLA Ops:
  5.6 8.8 %copy-start.13 = (s32[48,3]{0,1:T(4,128)S(1)}, s32[48,3]{0,1:T(4,128)}, u32[]{:S(2)}) copy-start(s32[48,3]{0,1:T(4,128)} %param.3) | copy-start | bytes 1732
  8.7 98.1 %collective-permute-start = (f32[432,1280]{1,0:T(8,128)}, f32[432,1280]{1,0:T(8,128)}, u32[]{:S(2)}, u32[]{:S(2)}) collective-permute-start(f32[432,1280]{1,0:T(8,128)} %constant_dynamic-slice_fusion.5), channel_id=1, source_target_pairs={{0,8},{8,0},{16,24},{24,16},{1,9},{9,1},{17,25},{25,17},{2,10},{10... | collective-permute-start | bytes 6635528 | tf_op jit(solution)/shard_map/ppermute | solution.py:295
  11.8 147.0 %collective-permute-start.1 = (f32[432,1280]{1,0:T(8,128)}, f32[432,1280]{1,0:T(8,128)}, u32[]{:S(2)}, u32[]{:S(2)}) collective-permute-start(f32[432,1280]{1,0:T(8,128)} %constant_dynamic-slice_fusion.6), channel_id=1, source_target_pairs={{0,16},{8,24},{16,0},{24,8},{1,17},{9,25},{17,1},{25,9},{2,18},{10... | collective-permute-start | bytes 6635528 | tf_op jit(solution)/shard_map/ppermute | solution.py:295
  14.4 144.4 %collective-permute-start.2 = (f32[432,1280]{1,0:T(8,128)S(1)}, f32[432,1280]{1,0:T(8,128)}, u32[]{:S(2)}, u32[]{:S(2)}) collective-permute-start(f32[432,1280]{1,0:T(8,128)S(1)} %constant_dynamic-slice_fusion.7), channel_id=1, source_target_pairs={{0,24},{8,16},{16,8},{24,0},{1,25},{9,17},{17,9},{25,1},{2,26},{10... | collective-permute-start | bytes 6635528 | tf_op jit(solution)/shard_map/ppermute | solution.py:295
  174.3 11.9 %collective-permute-start.3 = (f32[24,256,256]{2,1,0:T(8,128)}, f32[24,256,256]{2,1,0:T(8,128)}, u32[]{:S(2)}, u32[]{:S(2)}) collective-permute-start(f32[24,256,256]{2,1,0:T(8,128)} %get-tuple-element.100), channel_id=1, source_target_pairs={{0,2},{2,0},{4,6},{6,4},{1,3},{3,1},{5,7},{7,5},{8,10},{10,8},{12,... | collective-permute-start | bytes 18874376 | tf_op jit(solution)/shard_map/ppermute | solution.py:295
  193.1 49.6 %collective-permute-start.4 = (f32[1024,256]{1,0:T(8,128)}, f32[1024,256]{1,0:T(8,128)}, u32[]{:S(2)}, u32[]{:S(2)}) collective-permute-start(f32[1024,256]{1,0:T(8,128)} %get-tuple-element.101), channel_id=1, source_target_pairs={{0,4},{2,6},{4,0},{6,2},{1,5},{3,7},{5,1},{7,3},{8,12},{10,14},{12... | collective-permute-start | bytes 3145736 | tf_op jit(solution)/shard_map/ppermute | solution.py:295
  194.6 48.1 %collective-permute-start.5 = (f32[1024,256]{1,0:T(8,128)}, f32[1024,256]{1,0:T(8,128)}, u32[]{:S(2)}, u32[]{:S(2)}) collective-permute-start(f32[1024,256]{1,0:T(8,128)} %get-tuple-element.102), channel_id=1, source_target_pairs={{0,1},{1,0},{2,3},{3,2},{4,5},{5,4},{6,7},{7,6},{8,9},{9,8},{10,11... | collective-permute-start | bytes 3145736 | tf_op jit(solution)/shard_map/ppermute | solution.py:295
  196.1 70.2 %collective-permute-start.6 = (f32[1024,256]{1,0:T(8,128)}, f32[1024,256]{1,0:T(8,128)}, u32[]{:S(2)}, u32[]{:S(2)}) collective-permute-start(f32[1024,256]{1,0:T(8,128)} %get-tuple-element.103), channel_id=1, source_target_pairs={{0,8},{8,0},{16,24},{24,16},{1,9},{9,1},{17,25},{25,17},{2,10},{10... | collective-permute-start | bytes 3145736 | tf_op jit(solution)/shard_map/ppermute | solution.py:295
  268.7 19.3 %copy-start.7 = (f32[512,256]{1,0:T(8,128)S(1)}, f32[512,256]{1,0:T(8,128)}, u32[]{:S(2)}) copy-start(f32[512,256]{1,0:T(8,128)} %get-tuple-element.170) | copy-start | bytes 1572868
  273.0 13.4 %collective-permute-start.7 = (f32[512,256]{1,0:T(8,128)}, f32[512,256]{1,0:T(8,128)S(1)}, u32[]{:S(2)}, u32[]{:S(2)}) collective-permute-start(f32[512,256]{1,0:T(8,128)} %get-tuple-element.107), channel_id=1, source_target_pairs={{0,1},{1,0},{2,3},{3,2},{4,5},{5,4},{6,7},{7,6},{8,9},{9,8},{10,11... | collective-permute-start | bytes 1572872 | tf_op jit(solution)/shard_map/ppermute | solution.py:295
  273.5 13.1 %collective-permute-start.8 = (f32[512,256]{1,0:T(8,128)}, f32[512,256]{1,0:T(8,128)S(1)}, u32[]{:S(2)}, u32[]{:S(2)}) collective-permute-start(f32[512,256]{1,0:T(8,128)} %get-tuple-element.108), channel_id=1, source_target_pairs={{0,8},{8,0},{16,24},{24,16},{1,9},{9,1},{17,25},{25,17},{2,10},{10... | collective-permute-start | bytes 1572872 | tf_op jit(solution)/shard_map/ppermute | solution.py:295
  275.2 12.7 %collective-permute-start.9 = (f32[512,256]{1,0:T(8,128)}, f32[512,256]{1,0:T(8,128)}, u32[]{:S(2)}, u32[]{:S(2)}) collective-permute-start(f32[512,256]{1,0:T(8,128)} %get-tuple-element.109), channel_id=1, source_target_pairs={{0,4},{2,6},{4,0},{6,2},{1,5},{3,7},{5,1},{7,3},{8,12},{10,14},{12... | collective-permute-start | bytes 1572872 | tf_op jit(solution)/shard_map/ppermute | solution.py:295
  286.4 1.6 copy-start.12
  291.0 6.4 %collective-permute-start.10 = (f32[256,256]{1,0:T(8,128)S(1)}, f32[256,256]{1,0:T(8,128)S(1)}, u32[]{:S(2)}, u32[]{:S(2)}) collective-permute-start(f32[256,256]{1,0:T(8,128)S(1)} %get-tuple-element.113), channel_id=1, source_target_pairs={{0,8},{8,0},{16,24},{24,16},{1,9},{9,1},{17,25},{25,17},{2,10},{10... | collective-permute-start | bytes 786440 | tf_op jit(solution)/shard_map/ppermute | solution.py:295
  291.6 6.6 %collective-permute-start.11 = (f32[256,256]{1,0:T(8,128)}, f32[256,256]{1,0:T(8,128)S(1)}, u32[]{:S(2)}, u32[]{:S(2)}) collective-permute-start(f32[256,256]{1,0:T(8,128)} %get-tuple-element.114), channel_id=1, source_target_pairs={{0,4},{2,6},{4,0},{6,2},{1,5},{3,7},{5,1},{7,3},{8,12},{10,14},{12... | collective-permute-start | bytes 786440 | tf_op jit(solution)/shard_map/ppermute | solution.py:295
  292.2 6.4 %collective-permute-start.12 = (f32[256,256]{1,0:T(8,128)S(1)}, f32[256,256]{1,0:T(8,128)S(1)}, u32[]{:S(2)}, u32[]{:S(2)}) collective-permute-start(f32[256,256]{1,0:T(8,128)S(1)} %get-tuple-element.115), channel_id=1, source_target_pairs={{0,1},{1,0},{2,3},{3,2},{4,5},{5,4},{6,7},{7,6},{8,9},{9,8},{10,11... | collective-permute-start | bytes 786440 | tf_op jit(solution)/shard_map/ppermute | solution.py:295
  298.6 12.4 %collective-permute-start.13 = (f32[128,256]{1,0:T(8,128)S(1)}, f32[128,256]{1,0:T(8,128)S(1)}, u32[]{:S(2)}, u32[]{:S(2)}) collective-permute-start(f32[128,256]{1,0:T(8,128)S(1)} %dynamic-slice_add_fusion.20), channel_id=1, source_target_pairs={{0,16},{8,24},{16,0},{24,8},{1,17},{9,25},{17,1},{25,9},{2,18},{10... | collective-permute-start | bytes 393224 | tf_op jit(solution)/shard_map/ppermute | solution.py:295
  301.0 12.8 %collective-permute-start.14 = (f32[128,256]{1,0:T(8,128)S(1)}, f32[128,256]{1,0:T(8,128)S(1)}, u32[]{:S(2)}, u32[]{:S(2)}) collective-permute-start(f32[128,256]{1,0:T(8,128)S(1)} %dynamic-slice_add_fusion.19), channel_id=1, source_target_pairs={{0,16},{8,24},{16,0},{24,8},{1,17},{9,25},{17,1},{25,9},{2,18},{10... | collective-permute-start | bytes 393224 | tf_op jit(solution)/shard_map/ppermute | solution.py:295
  301.6 14.3 %collective-permute-start.15 = (f32[128,256]{1,0:T(8,128)S(1)}, f32[128,256]{1,0:T(8,128)S(1)}, u32[]{:S(2)}, u32[]{:S(2)}) collective-permute-start(f32[128,256]{1,0:T(8,128)S(1)} %dynamic-slice_add_fusion.18), channel_id=1, source_target_pairs={{0,16},{8,24},{16,0},{24,8},{1,17},{9,25},{17,1},{25,9},{2,18},{10... | collective-permute-start | bytes 393224 | tf_op jit(solution)/shard_map/ppermute | solution.py:295
  316.1 14.3 %collective-permute-start.16 = (f32[128,256]{1,0:T(8,128)S(1)}, f32[128,256]{1,0:T(8,128)S(1)}, u32[]{:S(2)}, u32[]{:S(2)}) collective-permute-start(f32[128,256]{1,0:T(8,128)S(1)} %add_add_fusion.2), channel_id=1, source_target_pairs={{0,16},{8,24},{16,0},{24,8},{1,17},{9,25},{17,1},{25,9},{2,18},{10... | collective-permute-start | bytes 393224 | tf_op jit(solution)/shard_map/ppermute | solution.py:295
  316.2 17.0 %collective-permute-start.17 = (f32[128,256]{1,0:T(8,128)S(1)}, f32[128,256]{1,0:T(8,128)S(1)}, u32[]{:S(2)}, u32[]{:S(2)}) collective-permute-start(f32[128,256]{1,0:T(8,128)S(1)} %add_add_fusion.1), channel_id=1, source_target_pairs={{0,16},{8,24},{16,0},{24,8},{1,17},{9,25},{17,1},{25,9},{2,18},{10... | collective-permute-start | bytes 393224 | tf_op jit(solution)/shard_map/ppermute | solution.py:295
  319.2 16.7 %collective-permute-start.18 = (f32[128,256]{1,0:T(8,128)S(1)}, f32[128,256]{1,0:T(8,128)S(1)}, u32[]{:S(2)}, u32[]{:S(2)}) collective-permute-start(f32[128,256]{1,0:T(8,128)S(1)} %add_add_fusion), channel_id=1, source_target_pairs={{0,16},{8,24},{16,0},{24,8},{1,17},{9,25},{17,1},{25,9},{2,18},{10... | collective-permute-start | bytes 393224 | tf_op jit(solution)/shard_map/ppermute | solution.py:295
  336.0 8.3 %collective-permute-start.19 = (f32[256,256]{1,0:T(8,128)S(1)}, f32[256,256]{1,0:T(8,128)S(1)}, u32[]{:S(2)}, u32[]{:S(2)}) collective-permute-start(f32[256,256]{1,0:T(8,128)S(1)} %constant_dynamic-update-slice_fusion.5), channel_id=1, source_target_pairs={{0,8},{8,0},{16,24},{24,16},{1,9},{9,1},{17,25},{25,17},{2,10},{10... | collective-permute-start | bytes 786440 | tf_op jit(solution)/shard_map/ppermute | solution.py:295
  336.0 8.3 %collective-permute-start.20 = (f32[256,256]{1,0:T(8,128)S(1)}, f32[256,256]{1,0:T(8,128)S(1)}, u32[]{:S(2)}, u32[]{:S(2)}) collective-permute-start(f32[256,256]{1,0:T(8,128)S(1)} %constant_dynamic-update-slice_fusion.2), channel_id=1, source_target_pairs={{0,4},{2,6},{4,0},{6,2},{1,5},{3,7},{5,1},{7,3},{8,12},{10,14},{12... | collective-permute-start | bytes 786440 | tf_op jit(solution)/shard_map/ppermute | solution.py:295
  337.6 7.9 %collective-permute-start.21 = (f32[256,256]{1,0:T(8,128)S(1)}, f32[256,256]{1,0:T(8,128)S(1)}, u32[]{:S(2)}, u32[]{:S(2)}) collective-permute-start(f32[256,256]{1,0:T(8,128)S(1)} %constant_dynamic-update-slice_fusion), channel_id=1, source_target_pairs={{0,1},{1,0},{2,3},{3,2},{4,5},{5,4},{6,7},{7,6},{8,9},{9,8},{10,11... | collective-permute-start | bytes 786440 | tf_op jit(solution)/shard_map/ppermute | solution.py:295
  345.7 12.8 %collective-permute-start.22 = (f32[512,256]{1,0:T(8,128)S(1)}, f32[512,256]{1,0:T(8,128)S(1)}, u32[]{:S(2)}, u32[]{:S(2)}) collective-permute-start(f32[512,256]{1,0:T(8,128)S(1)} %pad_maximum_fusion.3), channel_id=1, source_target_pairs={{0,1},{1,0},{2,3},{3,2},{4,5},{5,4},{6,7},{7,6},{8,9},{9,8},{10,11... | collective-permute-start | bytes 1572872 | tf_op jit(solution)/shard_map/ppermute | solution.py:295
  346.4 12.4 %collective-permute-start.23 = (f32[512,256]{1,0:T(8,128)S(1)}, f32[512,256]{1,0:T(8,128)S(1)}, u32[]{:S(2)}, u32[]{:S(2)}) collective-permute-start(f32[512,256]{1,0:T(8,128)S(1)} %pad_maximum_fusion.4), channel_id=1, source_target_pairs={{0,8},{8,0},{16,24},{24,16},{1,9},{9,1},{17,25},{25,17},{2,10},{10... | collective-permute-start | bytes 1572872 | tf_op jit(solution)/shard_map/ppermute | solution.py:295
  348.0 11.9 %collective-permute-start.24 = (f32[512,256]{1,0:T(8,128)S(1)}, f32[512,256]{1,0:T(8,128)S(1)}, u32[]{:S(2)}, u32[]{:S(2)}) collective-permute-start(f32[512,256]{1,0:T(8,128)S(1)} %pad_maximum_fusion.5), channel_id=1, source_target_pairs={{0,4},{2,6},{4,0},{6,2},{1,5},{3,7},{5,1},{7,3},{8,12},{10,14},{12... | collective-permute-start | bytes 1572872 | tf_op jit(solution)/shard_map/ppermute | solution.py:295
  360.1 22.3 %collective-permute-start.25 = (f32[1024,256]{1,0:T(8,128)S(1)}, f32[1024,256]{1,0:T(8,128)S(1)}, u32[]{:S(2)}, u32[]{:S(2)}) collective-permute-start(f32[1024,256]{1,0:T(8,128)S(1)} %pad_maximum_fusion), channel_id=1, source_target_pairs={{0,4},{2,6},{4,0},{6,2},{1,5},{3,7},{5,1},{7,3},{8,12},{10,14},{12... | collective-permute-start | bytes 3145736 | tf_op jit(solution)/shard_map/ppermute | solution.py:295
  360.8 22.0 %collective-permute-start.26 = (f32[1024,256]{1,0:T(8,128)S(1)}, f32[1024,256]{1,0:T(8,128)S(1)}, u32[]{:S(2)}, u32[]{:S(2)}) collective-permute-start(f32[1024,256]{1,0:T(8,128)S(1)} %pad_maximum_fusion.1), channel_id=1, source_target_pairs={{0,1},{1,0},{2,3},{3,2},{4,5},{5,4},{6,7},{7,6},{8,9},{9,8},{10,11... | collective-permute-start | bytes 3145736 | tf_op jit(solution)/shard_map/ppermute | solution.py:295
  362.2 21.7 %collective-permute-start.27 = (f32[1024,256]{1,0:T(8,128)S(1)}, f32[1024,256]{1,0:T(8,128)S(1)}, u32[]{:S(2)}, u32[]{:S(2)}) collective-permute-start(f32[1024,256]{1,0:T(8,128)S(1)} %pad_maximum_fusion.2), channel_id=1, source_target_pairs={{0,8},{8,0},{16,24},{24,16},{1,9},{9,1},{17,25},{25,17},{2,10},{10... | collective-permute-start | bytes 3145736 | tf_op jit(solution)/shard_map/ppermute | solution.py:295
  363.1 21.0 %copy-start.1 = (f32[3072,256]{1,0:T(8,128)}, f32[3072,256]{1,0:T(8,128)S(1)}, u32[]{:S(2)}) copy-start(f32[3072,256]{1,0:T(8,128)S(1)} %constant_dynamic-update-slice_fusion.6) | copy-start | bytes 9437188
  363.1 22.9 %collective-permute-start.28 = (f32[3072,256]{1,0:T(8,128)S(1)}, f32[3072,256]{1,0:T(8,128)S(1)}, u32[]{:S(2)}, u32[]{:S(2)}) collective-permute-start(f32[3072,256]{1,0:T(8,128)S(1)} %constant_dynamic-update-slice_fusion.6), channel_id=1, source_target_pairs={{0,2},{2,0},{4,6},{6,4},{1,3},{3,1},{5,7},{7,5},{8,10},{10,8},{12,... | collective-permute-start | bytes 9437192 | tf_op jit(solution)/shard_map/ppermute | solution.py:295
  384.0 7.4 %copy-start = (f32[3072,256]{1,0:T(8,128)}, f32[3072,256]{1,0:T(8,128)S(1)}, u32[]{:S(2)}) copy-start(f32[3072,256]{1,0:T(8,128)S(1)} %constant_dynamic-update-slice_fusion.9) | copy-start | bytes 9437188
  384.0 5.7 collective-permute-start.29
  386.0 3.8 copy-start.2
  389.7 1.7 copy-start.3
  391.4 19.0 %copy-start.11 = (f32[144,1280]{1,0:T(8,128)S(1)}, f32[144,1280]{1,0:T(8,128)}, u32[]{:S(2)}) copy-start(f32[144,1280]{1,0:T(8,128)} %constant_dynamic-slice_fusion.2) | copy-start | bytes 2211844
  391.5 19.1 %copy-start.10 = (f32[144,1280]{1,0:T(8,128)S(1)}, f32[144,1280]{1,0:T(8,128)}, u32[]{:S(2)}) copy-start(f32[144,1280]{1,0:T(8,128)} %constant_dynamic-slice_fusion.1) | copy-start | bytes 2211844
  407.0 191.0 %collective-permute-start.35 = (f32[432,1280]{1,0:T(8,128)}, f32[432,1280]{1,0:T(8,128)}, u32[]{:S(2)}, u32[]{:S(2)}) collective-permute-start(f32[432,1280]{1,0:T(8,128)} %eager.5), channel_id=1, source_target_pairs={{0,8},{8,0},{16,24},{24,16},{1,9},{9,1},{17,25},{25,17},{2,10},{10... | collective-permute-start | bytes 6635528 | tf_op jit(solution)/shard_map/ppermute | solution.py:295
  410.4 127.6 %collective-permute-start.31 = (f32[144,1280]{1,0:T(8,128)S(1)}, f32[144,1280]{1,0:T(8,128)S(1)}, u32[]{:S(2)}, u32[]{:S(2)}) collective-permute-start(f32[144,1280]{1,0:T(8,128)S(1)} %copy-done.11), channel_id=1, source_target_pairs={{0,8},{8,0},{16,24},{24,16},{1,9},{9,1},{17,25},{25,17},{2,10},{10... | collective-permute-start | bytes 2211848 | tf_op jit(solution)/shard_map/ppermute | solution.py:295
  410.5 127.5 %collective-permute-start.32 = (f32[144,1280]{1,0:T(8,128)S(1)}, f32[144,1280]{1,0:T(8,128)S(1)}, u32[]{:S(2)}, u32[]{:S(2)}) collective-permute-start(f32[144,1280]{1,0:T(8,128)S(1)} %copy-done.10), channel_id=1, source_target_pairs={{0,16},{8,24},{16,0},{24,8},{1,17},{9,25},{17,1},{25,9},{2,18},{10... | collective-permute-start | bytes 2211848 | tf_op jit(solution)/shard_map/ppermute | solution.py:295
  410.5 127.5 %collective-permute-start.33 = (f32[144,1280]{1,0:T(8,128)}, f32[144,1280]{1,0:T(8,128)S(1)}, u32[]{:S(2)}, u32[]{:S(2)}) collective-permute-start(f32[144,1280]{1,0:T(8,128)} %constant_dynamic-slice_fusion), channel_id=1, source_target_pairs={{0,24},{8,16},{16,8},{24,0},{1,25},{9,17},{17,9},{25,1},{2,26},{10... | collective-permute-start | bytes 2211848 | tf_op jit(solution)/shard_map/ppermute | solution.py:295
  427.5 166.4 %collective-permute-start.36 = (f32[288,1280]{1,0:T(8,128)}, f32[288,1280]{1,0:T(8,128)S(1)}, u32[]{:S(2)}, u32[]{:S(2)}) collective-permute-start(f32[288,1280]{1,0:T(8,128)} %eager.6), channel_id=1, source_target_pairs={{0,24},{8,16},{16,8},{24,0},{1,25},{9,17},{17,9},{25,1},{2,26},{10... | collective-permute-start | bytes 4423688 | tf_op jit(solution)/shard_map/ppermute | solution.py:295
  538.0 67.7 %collective-permute-start.30 = (f32[288,1280]{1,0:T(8,128)}, f32[288,1280]{1,0:T(8,128)S(1)}, u32[]{:S(2)}, u32[]{:S(2)}) collective-permute-start(f32[288,1280]{1,0:T(8,128)} %eager.4), channel_id=1, source_target_pairs={{0,16},{8,24},{16,0},{24,8},{1,17},{9,25},{17,1},{25,9},{2,18},{10... | collective-permute-start | bytes 4423688 | tf_op jit(solution)/shard_map/ppermute | solution.py:295
  538.0 1.2 copy-start.5
  553.5 49.7 %collective-permute-start.34 = (f32[144,1280]{1,0:T(8,128)}, f32[144,1280]{1,0:T(8,128)}, u32[]{:S(2)}, u32[]{:S(2)}) collective-permute-start(f32[144,1280]{1,0:T(8,128)} %correction.2), channel_id=1, source_target_pairs={{0,8},{8,0},{16,24},{24,16},{1,9},{9,1},{17,25},{25,17},{2,10},{10... | collective-permute-start | bytes 2211848 | tf_op jit(solution)/shard_map/ppermute | solution.py:295
  605.7 1.1 copy-start.8
  (3 other events, 2.9 us)

commit v4 on v3

--- a/solution.py
+++ b/solution.py
@@ -201,7 +201,7 @@
     )(at[None] // block, part, weight, *earlier)
 
 
-def eager_kernel(parts, per, table, *refs):
+def eager_kernel(parts, per, begin, table, *refs):
     grams = refs[:parts]
     high, low, out, held, high_here, low_here, gram_sem, side_sem = refs[parts:]
     slots, rows, _ = high_here.shape
@@ -210,7 +210,7 @@
     def sides(g):
         part = pl.ds(g * per, per)
         return [
-            pltpu.make_async_copy(far.at[part, pl.ds(0, rows)], near.at[part], side_sem.at[which, g])
+            pltpu.make_async_copy(far.at[part, pl.ds(begin, rows)], near.at[part], side_sem.at[which, g])
             for which, (far, near) in enumerate(((high, high_here), (low, low_here)))
         ]
 
@@ -256,10 +256,10 @@
     each(add)
 
 
-def eager_call(table, grams, arrays, rows, per):
+def eager_call(table, grams, arrays, begin, rows, per):
     slots, count = arrays[0].shape[0], table.shape[0]
     return pl.pallas_call(
-        functools.partial(eager_kernel, len(grams), per),
+        functools.partial(eager_kernel, len(grams), per, begin),
         grid_spec=pltpu.PrefetchScalarGridSpec(
             num_scalar_prefetch=1,
             grid=(1,),
@@ -406,9 +406,11 @@
         for d in range(n):
             chunk = lax.dynamic_slice_in_dim(source, (z ^ d ^ top) * rows + less, more, 0)
             source, chunk = together((source, chunk))
+            if 0 < d < top:
+                chunk = flip(chunk, ("tri", d))
             mirrored.append(chunk)
         pieces, mirrored = together((pieces, mirrored))
-        mirrored = [flip(chunk, ("tri", d)) if d else chunk for d, chunk in enumerate(mirrored)]
+        mirrored = mirrored[:top] + [flip(mirrored[d], ("tri", d)) for d in range(top, n)]
 
     sent, *panels = gram_call(where_sent, pieces, 1.0 / columns, True)
     got = flip(sent, core_dim)
@@ -422,17 +424,24 @@
     grams = [g.reshape(count // 4, PANEL, PANEL) for g in (here, there, here_other, there_other)]
 
     ready = [[], [], [], []]
+    part, turn = grams[0], 0
     for d in range(n - 1, -1, -1):
-        found = [((z ^ d) * rows, eager_call(tables[d], grams, panels, less if d >= top else rows, per))]
+        size = less if d >= top else rows
+        jobs = [(eager_call, (panels, 0, size), z ^ d, 0, size)]
         if more and d < top:
-            found.append(((z ^ d ^ top) * rows + less, correction_call(tables[d], grams, mirrored, more, per)))
+            jobs.append((correction_call, (mirrored, more), z ^ d ^ top, less, more))
         when = 0 if d == 0 else 1 if d > top else 3 if d == top else 2
-        ready[when] += [(at, flip(part, ("tri", d)) if d else part) for at, part in found]
-    ready = sum(ready, [])
-
-    block = math.gcd(rows, more)
+        for call, how, chunk, start, size in jobs:
+            table, _ = together((tables[d], part))
+            part = call(table, grams, *how, per)
+            sent = flip(part, ("tri", d)) if d else part
+            turn += 1
+            block = math.gcd(rows, math.gcd(start, size))
+            block = block // 3 if block == rows and rows % 24 == 0 else block
+            ready[when].append((chunk * rows + start, sent, block))
+
     placed = ()
-    for at, part in ready:
+    for at, part, block in sum(ready, []):
         placed = place_call(at, part, padded, placed, block)
     correction, updated = placed
     return correction[:local], updated[:local]

time: 611 us -> 631 us (1.033)
  waiting for transfers between devices: 340 us -> 371 us
  starting transfers between devices: 87.7 us -> 75.6 us
    ppermute x37, waiting for transfers between devices: 340 us -> 371 us  [flip(): return lax.ppermute(value, axis, pairs)]
    ppermute x37, starting transfers between devices: 87.7 us -> 75.6 us  [flip(): return lax.ppermute(value, axis, pairs)]
  transfers between devices with their start and end apart: 37 -> 37, of which waited for: 26 -> 27; matrix products, arithmetic and copies ran while one was open for 3% -> 3% of each run, Pallas kernels for 17% -> 12%
where the time goes in v4:
time: 631 us; the launch traced here: 630 us
  waiting for transfers between devices  371 us (59%)
  Pallas kernels  135 us (21%)
  starting transfers between devices  75.6 us (12%)
  local copies, waits for them, and re-layouts  30.3 us (5%)
  other arithmetic  17.4 us (3%)
    ppermute x37, waiting for transfers between devices, flip(): return lax.ppermute(value, axis, pairs)  371 us
    ppermute x37, starting transfers between devices, flip(): return lax.ppermute(value, axis, pairs)  75.6 us
    pallas_call x4, Pallas kernels, eager_call(): pl.pallas_call(functools.partial(eager_kernel, len(grams), per, begin), g...  58.4 us
    pallas_call x2, Pallas kernels, correction_call(): pl.pallas_call(functools.partial(correction_kernel, len(grams), len(array...  27.7 us
    pallas_call x2, Pallas kernels, gram_call(): pl.pallas_call(functools.partial(gram_first_kernel, scale, n, slots // n)...  27.4 us
    pallas_call x6, Pallas kernels, place_call(): pl.pallas_call(place_kernel, grid_spec=pltpu.PrefetchScalarGridSpec(num_s...  21.4 us
    add x10, other arithmetic, cut(): sum((lax.dynamic_slice_in_dim(t, base + start, rows, 0) for base, t in te...  15.7 us
  transfers between devices with their start and end apart: 37, of which 27 were waited for; matrix products, arithmetic and copies ran while one was open for 3% of the time, Pallas kernels for 12%

profile of v4, /device:TPU:0, one launch (start us, length us, event | category | flops | bytes accessed | tf_op | source)
XLA Modules:
  0.0 629.8 jit_solution(1910995856264081118)
XLA Ops:
  2.4 3.2 constant_dynamic-slice_fusion.6
  5.6 3.1 constant_dynamic-slice_fusion.5
  8.7 3.1 collective-permute-start
  11.8 2.6 collective-permute-start.1
  14.4 2.0 constant_dynamic-slice_fusion.3.refs_4_
  19.5 2.0 constant_dynamic-slice_fusion.1
  21.5 2.0 constant_dynamic-slice_fusion
  25.2 3.1 constant_dynamic-slice_fusion.4.refs_0_
  28.3 142.4 %collective-permute-done.3.refs_5_ = f32[144,1280]{1,0:T(8,128)S(1)} collective-permute-done((f32[144,1280]{1,0:T(8,128)}, f32[144,1280]{1,0:T(8,128)S(1)}, u32[]{:S(2)}, u32[]{:S(2)}) %collective-permute-start.3) | collective-permute-done | bytes 737312 | tf_op jit(solution)/shard_map/ppermute | solution.py:295
  170.7 15.6 %gram_first.1 = (f32[24,256,256]{2,1,0:T(8,128)}, bf16[20,432,256]{2,1,0:T(8,128)(2,1)}, bf16[20,432,256]{2,1,0:T(8,128)(2,1)}) custom-call(s32[24,2]{1,0:T(8,128)} %get-tuple-element.193.where, f32[432,1280]{1,0:T(8,128)} %constant_dynamic-slice_fusion.4.refs_0_, f32[432,1280]{1,0:T(8,128)} %collective-permute-done.refs_1_, ...), custom_call_target="tpu_custom_call" | custom-call | flops 4076863488 | bytes 23986176 | tf_op jit(solution)/shard_map/gram_first/pallas_call | solution.py:73
  186.3 11.9 %gram.1 = f32[24,256,256]{2,1,0:T(8,128)} custom-call(s32[24,2]{1,0:T(8,128)} %get-tuple-element.192.where, bf16[20,432,256]{2,1,0:T(8,128)(2,1)} %get-tuple-element.104.high.refs_4_, bf16[20,432,256]{2,1,0:T(8,128)(2,1)} %get-tuple-element.105.low.refs_5_), custom_call_target="tpu_custom_call" | custom-call | flops 4076863488 | bytes 23986176 | tf_op jit(solution)/shard_map/gram/pallas_call | solution.py:73
  198.2 6.9 %dynamic-slice_add_fusion = (f32[1024,256]{1,0:T(8,128)S(1)}, f32[1024,256]{1,0:T(8,128)S(1)}, f32[1024,256]{1,0:T(8,128)}, f32[1024,256]{1,0:T(8,128)}, f32[1024,256]{1,0:T(8,128)}, /*index=5*/f32[1024,256]{1,0:T(8,128)S(1)}) fusion(f32[6144,256]{1,0:T(8,128)} %bitcast.3, s32[]{:T(128)S(6)} %select_n.592, f32[6144,256]{1,0:T(8,128)} %bitcast.24, ...), kind=kLoop, calls=%fused_computation.4 | loop fusion | flops 1572864 | bytes 18874392 | tf_op jit(solution)/shard_map/add | solution.py:312
  208.3 34.6 %collective-permute-start.7 = (f32[1024,256]{1,0:T(8,128)}, f32[1024,256]{1,0:T(8,128)}, u32[]{:S(2)}, u32[]{:S(2)}) collective-permute-start(f32[1024,256]{1,0:T(8,128)} %get-tuple-element.109), channel_id=1, source_target_pairs={{0,8},{8,0},{16,24},{24,16},{1,9},{9,1},{17,25},{25,17},{2,10},{10... | collective-permute-start | bytes 3145736 | tf_op jit(solution)/shard_map/ppermute | solution.py:295
  242.8 23.5 %collective-permute-done.7 = f32[1024,256]{1,0:T(8,128)} collective-permute-done((f32[1024,256]{1,0:T(8,128)}, f32[1024,256]{1,0:T(8,128)}, u32[]{:S(2)}, u32[]{:S(2)}) %collective-permute-start.7) | collective-permute-done | bytes 1048608 | tf_op jit(solution)/shard_map/ppermute | solution.py:295
  266.4 2.3 dynamic-slice_add_fusion.6
  268.7 2.2 dynamic-slice_add_fusion.11
  275.0 10.7 %collective-permute-done.8 = f32[512,256]{1,0:T(8,128)} collective-permute-done((f32[512,256]{1,0:T(8,128)}, f32[512,256]{1,0:T(8,128)}, u32[]{:S(2)}, u32[]{:S(2)}) %collective-permute-start.8) | collective-permute-done | bytes 524320 | tf_op jit(solution)/shard_map/ppermute | solution.py:295
  292.7 3.8 collective-permute-done.11
  297.7 2.5 collective-permute-start.14
  300.6 2.5 collective-permute-start.16
  303.1 6.7 %collective-permute-done.14 = f32[128,256]{1,0:T(8,128)S(1)} collective-permute-done((f32[128,256]{1,0:T(8,128)S(1)}, f32[128,256]{1,0:T(8,128)S(1)}, u32[]{:S(2)}, u32[]{:S(2)}) %collective-permute-start.14) | collective-permute-done | bytes 131104 | tf_op jit(solution)/shard_map/ppermute | solution.py:295
  309.9 2.8 collective-permute-done.15
  314.8 3.0 collective-permute-start.18
  317.9 10.6 %collective-permute-done.17 = f32[128,256]{1,0:T(8,128)S(1)} collective-permute-done((f32[128,256]{1,0:T(8,128)S(1)}, f32[128,256]{1,0:T(8,128)S(1)}, u32[]{:S(2)}, u32[]{:S(2)}) %collective-permute-start.17) | collective-permute-done | bytes 131104 | tf_op jit(solution)/shard_map/ppermute | solution.py:295
  328.5 2.8 collective-permute-done.18
  331.3 2.7 collective-permute-done.19
  337.4 5.0 collective-permute-done.20
  347.8 8.9 %collective-permute-done.23 = f32[512,256]{1,0:T(8,128)S(1)} collective-permute-done((f32[512,256]{1,0:T(8,128)S(1)}, f32[512,256]{1,0:T(8,128)S(1)}, u32[]{:S(2)}, u32[]{:S(2)}) %collective-permute-start.23) | collective-permute-done | bytes 524320 | tf_op jit(solution)/shard_map/ppermute | solution.py:295
  364.2 17.5 %collective-permute-done.26 = f32[1024,256]{1,0:T(8,128)S(1)} collective-permute-done((f32[1024,256]{1,0:T(8,128)S(1)}, f32[1024,256]{1,0:T(8,128)S(1)}, u32[]{:S(2)}, u32[]{:S(2)}) %collective-permute-start.26) | collective-permute-done | bytes 1048608 | tf_op jit(solution)/shard_map/ppermute | solution.py:295
  384.0 4.1 collective-permute-done.30
  388.1 12.7 %eager.4 = f32[288,1280]{1,0:T(8,128)} custom-call(s32[48,4]{1,0:T(8,128)} %copy.60.table, f32[12,256,256]{2,1,0:T(8,128)} %bitcast.4.refs_0_, f32[12,256,256]{2,1,0:T(8,128)} %bitcast.18, f32[12,256,256]{2,1,0:T(8,128)} %bitcast.6.refs_2_, f32[12,256,256]{2,1,0:T(8,128)} %bitcast.7.refs_3_, bf16[20,432,256]{2,1,0:T(8,128)(2,1)} %get-tuple-element.104.high.refs_4_, ...), custom_call_target="tpu_custom_call" | custom-call | flops 2717908992 | bytes 18481152 | tf_op jit(solution)/shard_map/eager/pallas_call | solution.py:261
  401.4 12.3 %eager.5 = f32[288,1280]{1,0:T(8,128)} custom-call(s32[48,4]{1,0:T(8,128)} %copy.61.table, f32[12,256,256]{2,1,0:T(8,128)} %bitcast.4.refs_0_, f32[12,256,256]{2,1,0:T(8,128)} %bitcast.19, f32[12,256,256]{2,1,0:T(8,128)} %bitcast.6.refs_2_, f32[12,256,256]{2,1,0:T(8,128)} %bitcast.7.refs_3_, bf16[20,432,256]{2,1,0:T(8,128)(2,1)} %get-tuple-element.104.high.refs_4_, ...), custom_call_target="tpu_custom_call" | custom-call | flops 2717908992 | bytes 18481152 | tf_op jit(solution)/shard_map/eager/pallas_call | solution.py:261
  414.4 15.6 %eager.6 = f32[432,1280]{1,0:T(8,128)} custom-call(s32[48,4]{1,0:T(8,128)} %copy.66.table, f32[12,256,256]{2,1,0:T(8,128)} %bitcast.4.refs_0_, f32[12,256,256]{2,1,0:T(8,128)} %bitcast.20, f32[12,256,256]{2,1,0:T(8,128)} %bitcast.6.refs_2_, f32[12,256,256]{2,1,0:T(8,128)} %bitcast.7.refs_3_, bf16[20,432,256]{2,1,0:T(8,128)(2,1)} %get-tuple-element.104.high.refs_4_, ...), custom_call_target="tpu_custom_call" | custom-call | flops 4076863488 | bytes 21430272 | tf_op jit(solution)/shard_map/eager/pallas_call | solution.py:261
  430.0 3.4 collective-permute-start.35
  435.9 2.3 collective-permute-start.36
  439.1 59.0 %collective-permute-done.32.refs_6_ = f32[144,1280]{1,0:T(8,128)S(1)} collective-permute-done((f32[144,1280]{1,0:T(8,128)}, f32[144,1280]{1,0:T(8,128)S(1)}, u32[]{:S(2)}, u32[]{:S(2)}) %collective-permute-start.32) | collective-permute-done | bytes 737312 | tf_op jit(solution)/shard_map/ppermute | solution.py:295
  498.1 18.1 %collective-permute-done.33.refs_7_ = f32[144,1280]{1,0:T(8,128)S(1)} collective-permute-done((f32[144,1280]{1,0:T(8,128)}, f32[144,1280]{1,0:T(8,128)S(1)}, u32[]{:S(2)}, u32[]{:S(2)}) %collective-permute-start.33) | collective-permute-done | bytes 737312 | tf_op jit(solution)/shard_map/ppermute | solution.py:295
  517.1 13.4 %correction.2 = f32[144,1280]{1,0:T(8,128)} custom-call(s32[48,4]{1,0:T(8,128)} %copy.67.table, f32[12,256,256]{2,1,0:T(8,128)} %bitcast.4.refs_0_, f32[12,256,256]{2,1,0:T(8,128)} %bitcast.21, f32[12,256,256]{2,1,0:T(8,128)} %bitcast.6.refs_2_, f32[12,256,256]{2,1,0:T(8,128)} %bitcast.7.refs_3_, f32[144,1280]{1,0:T(8,128)} %constant_dynamic-slice_fusion.3.refs_4_, ...), custom_call_target="tpu_custom_call" | custom-call | flops 1358954496 | bytes 15532032 | tf_op jit(solution)/shard_map/correction/pallas_call | solution.py:155
  531.2 17.8 %eager.7.part = f32[432,1280]{1,0:T(8,128)} custom-call(s32[48,4]{1,0:T(8,128)} %copy.72.table, f32[12,256,256]{2,1,0:T(8,128)} %bitcast.4.refs_0_, f32[12,256,256]{2,1,0:T(8,128)} %bitcast.22, f32[12,256,256]{2,1,0:T(8,128)} %bitcast.6.refs_2_, f32[12,256,256]{2,1,0:T(8,128)} %bitcast.7.refs_3_, bf16[20,432,256]{2,1,0:T(8,128)(2,1)} %get-tuple-element.104.high.refs_4_, ...), custom_call_target="tpu_custom_call" | custom-call | flops 4076863488 | bytes 21430272 | tf_op jit(solution)/shard_map/eager/pallas_call | solution.py:261
  549.7 5.2 place.6
  554.9 14.3 %correction.3.part = f32[144,1280]{1,0:T(8,128)} custom-call(s32[48,4]{1,0:T(8,128)} %copy.73.table, f32[12,256,256]{2,1,0:T(8,128)} %bitcast.4.refs_0_, f32[12,256,256]{2,1,0:T(8,128)} %bitcast.23, f32[12,256,256]{2,1,0:T(8,128)} %bitcast.6.refs_2_, f32[12,256,256]{2,1,0:T(8,128)} %bitcast.7.refs_3_, f32[144,1280]{1,0:T(8,128)} %constant_dynamic-slice_fusion.3.refs_4_, ...), custom_call_target="tpu_custom_call" | custom-call | flops 1358954496 | bytes 15532032 | tf_op jit(solution)/shard_map/correction/pallas_call | solution.py:155
  569.2 2.5 place.7
  571.7 3.1 place.8
  574.8 5.2 place.9
  579.9 12.2 %collective-permute-done.34.part = f32[144,1280]{1,0:T(8,128)S(1)} collective-permute-done((f32[144,1280]{1,0:T(8,128)}, f32[144,1280]{1,0:T(8,128)S(1)}, u32[]{:S(2)}, u32[]{:S(2)}) %collective-permute-start.34) | collective-permute-done | bytes 737312 | tf_op jit(solution)/shard_map/ppermute | solution.py:295
  593.0 2.5 place.10
  595.5 31.3 %collective-permute-done.31.part = f32[288,1280]{1,0:T(8,128)} collective-permute-done((f32[288,1280]{1,0:T(8,128)S(1)}, f32[288,1280]{1,0:T(8,128)}, u32[]{:S(2)}, u32[]{:S(2)}) %collective-permute-start.31) | collective-permute-done | bytes 1474592 | tf_op jit(solution)/shard_map/ppermute | solution.py:295
  626.8 3.0 place.11
  (123 shorter events, 51.0 us)
Async XLA Ops:
  5.6 13.8 %copy-start.7 = (s32[48,3]{0,1:T(4,128)S(1)}, s32[48,3]{0,1:T(4,128)}, u32[]{:S(2)}) copy-start(s32[48,3]{0,1:T(4,128)} %param.3) | copy-start | bytes 1732
  8.7 162.0 %collective-permute-start = (f32[432,1280]{1,0:T(8,128)}, f32[432,1280]{1,0:T(8,128)}, u32[]{:S(2)}, u32[]{:S(2)}) collective-permute-start(f32[432,1280]{1,0:T(8,128)} %constant_dynamic-slice_fusion.5), channel_id=1, source_target_pairs={{0,8},{8,0},{16,24},{24,16},{1,9},{9,1},{17,25},{25,17},{2,10},{10... | collective-permute-start | bytes 6635528 | tf_op jit(solution)/shard_map/ppermute | solution.py:295
  11.8 158.9 %collective-permute-start.1 = (f32[432,1280]{1,0:T(8,128)}, f32[432,1280]{1,0:T(8,128)}, u32[]{:S(2)}, u32[]{:S(2)}) collective-permute-start(f32[432,1280]{1,0:T(8,128)} %constant_dynamic-slice_fusion.6), channel_id=1, source_target_pairs={{0,16},{8,24},{16,0},{24,8},{1,17},{9,25},{17,1},{25,9},{2,18},{10... | collective-permute-start | bytes 6635528 | tf_op jit(solution)/shard_map/ppermute | solution.py:295
  14.4 156.3 %collective-permute-start.2 = (f32[432,1280]{1,0:T(8,128)S(1)}, f32[432,1280]{1,0:T(8,128)}, u32[]{:S(2)}, u32[]{:S(2)}) collective-permute-start(f32[432,1280]{1,0:T(8,128)S(1)} %constant_dynamic-slice_fusion.7), channel_id=1, source_target_pairs={{0,24},{8,16},{16,8},{24,0},{1,25},{9,17},{17,9},{25,1},{2,26},{10... | collective-permute-start | bytes 6635528 | tf_op jit(solution)/shard_map/ppermute | solution.py:295
  18.5 152.2 %collective-permute-start.3 = (f32[144,1280]{1,0:T(8,128)}, f32[144,1280]{1,0:T(8,128)S(1)}, u32[]{:S(2)}, u32[]{:S(2)}) collective-permute-start(f32[144,1280]{1,0:T(8,128)} %constant_dynamic-slice_fusion.2), channel_id=1, source_target_pairs={{0,8},{8,0},{16,24},{24,16},{1,9},{9,1},{17,25},{25,17},{2,10},{10... | collective-permute-start | bytes 2211848 | tf_op jit(solution)/shard_map/ppermute | solution.py:295
  170.7 15.6 %copy-start.1 = (f32[144,1280]{1,0:T(8,128)}, f32[144,1280]{1,0:T(8,128)S(1)}, u32[]{:S(2)}) copy-start(f32[144,1280]{1,0:T(8,128)S(1)} %collective-permute-done.3.refs_5_) | copy-start | bytes 2211844
  186.3 11.9 %collective-permute-start.4 = (f32[24,256,256]{2,1,0:T(8,128)}, f32[24,256,256]{2,1,0:T(8,128)}, u32[]{:S(2)}, u32[]{:S(2)}) collective-permute-start(f32[24,256,256]{2,1,0:T(8,128)} %get-tuple-element.106), channel_id=1, source_target_pairs={{0,2},{2,0},{4,6},{6,4},{1,3},{3,1},{5,7},{7,5},{8,10},{10,8},{12,... | collective-permute-start | bytes 18874376 | tf_op jit(solution)/shard_map/ppermute | solution.py:295
  205.1 37.7 %collective-permute-start.5 = (f32[1024,256]{1,0:T(8,128)}, f32[1024,256]{1,0:T(8,128)}, u32[]{:S(2)}, u32[]{:S(2)}) collective-permute-start(f32[1024,256]{1,0:T(8,128)} %get-tuple-element.107), channel_id=1, source_target_pairs={{0,4},{2,6},{4,0},{6,2},{1,5},{3,7},{5,1},{7,3},{8,12},{10,14},{12... | collective-permute-start | bytes 3145736 | tf_op jit(solution)/shard_map/ppermute | solution.py:295
  206.7 36.1 %collective-permute-start.6 = (f32[1024,256]{1,0:T(8,128)}, f32[1024,256]{1,0:T(8,128)}, u32[]{:S(2)}, u32[]{:S(2)}) collective-permute-start(f32[1024,256]{1,0:T(8,128)} %get-tuple-element.108), channel_id=1, source_target_pairs={{0,1},{1,0},{2,3},{3,2},{4,5},{5,4},{6,7},{7,6},{8,9},{9,8},{10,11... | collective-permute-start | bytes 3145736 | tf_op jit(solution)/shard_map/ppermute | solution.py:295
  208.3 58.1 %collective-permute-start.7 = (f32[1024,256]{1,0:T(8,128)}, f32[1024,256]{1,0:T(8,128)}, u32[]{:S(2)}, u32[]{:S(2)}) collective-permute-start(f32[1024,256]{1,0:T(8,128)} %get-tuple-element.109), channel_id=1, source_target_pairs={{0,8},{8,0},{16,24},{24,16},{1,9},{9,1},{17,25},{25,17},{2,10},{10... | collective-permute-start | bytes 3145736 | tf_op jit(solution)/shard_map/ppermute | solution.py:295
  268.6 18.5 %copy-start.4 = (f32[512,256]{1,0:T(8,128)S(1)}, f32[512,256]{1,0:T(8,128)}, u32[]{:S(2)}) copy-start(f32[512,256]{1,0:T(8,128)} %get-tuple-element.180) | copy-start | bytes 1572868
  272.2 13.5 %collective-permute-start.8 = (f32[512,256]{1,0:T(8,128)}, f32[512,256]{1,0:T(8,128)}, u32[]{:S(2)}, u32[]{:S(2)}) collective-permute-start(f32[512,256]{1,0:T(8,128)} %get-tuple-element.113), channel_id=1, source_target_pairs={{0,1},{1,0},{2,3},{3,2},{4,5},{5,4},{6,7},{7,6},{8,9},{9,8},{10,11... | collective-permute-start | bytes 1572872 | tf_op jit(solution)/shard_map/ppermute | solution.py:295
  272.7 13.0 %collective-permute-start.9 = (f32[512,256]{1,0:T(8,128)S(1)}, f32[512,256]{1,0:T(8,128)S(1)}, u32[]{:S(2)}, u32[]{:S(2)}) collective-permute-start(f32[512,256]{1,0:T(8,128)S(1)} %get-tuple-element.114), channel_id=1, source_target_pairs={{0,8},{8,0},{16,24},{24,16},{1,9},{9,1},{17,25},{25,17},{2,10},{10... | collective-permute-start | bytes 1572872 | tf_op jit(solution)/shard_map/ppermute | solution.py:295
  274.5 12.7 %collective-permute-start.10 = (f32[512,256]{1,0:T(8,128)}, f32[512,256]{1,0:T(8,128)}, u32[]{:S(2)}, u32[]{:S(2)}) collective-permute-start(f32[512,256]{1,0:T(8,128)} %get-tuple-element.115), channel_id=1, source_target_pairs={{0,4},{2,6},{4,0},{6,2},{1,5},{3,7},{5,1},{7,3},{8,12},{10,14},{12... | collective-permute-start | bytes 1572872 | tf_op jit(solution)/shard_map/ppermute | solution.py:295
  290.2 6.4 %collective-permute-start.11 = (f32[256,256]{1,0:T(8,128)S(1)}, f32[256,256]{1,0:T(8,128)S(1)}, u32[]{:S(2)}, u32[]{:S(2)}) collective-permute-start(f32[256,256]{1,0:T(8,128)S(1)} %get-tuple-element.119), channel_id=1, source_target_pairs={{0,8},{8,0},{16,24},{24,16},{1,9},{9,1},{17,25},{25,17},{2,10},{10... | collective-permute-start | bytes 786440 | tf_op jit(solution)/shard_map/ppermute | solution.py:295
  290.7 6.6 %collective-permute-start.12 = (f32[256,256]{1,0:T(8,128)}, f32[256,256]{1,0:T(8,128)S(1)}, u32[]{:S(2)}, u32[]{:S(2)}) collective-permute-start(f32[256,256]{1,0:T(8,128)} %get-tuple-element.120), channel_id=1, source_target_pairs={{0,4},{2,6},{4,0},{6,2},{1,5},{3,7},{5,1},{7,3},{8,12},{10,14},{12... | collective-permute-start | bytes 786440 | tf_op jit(solution)/shard_map/ppermute | solution.py:295
  291.2 6.4 %collective-permute-start.13 = (f32[256,256]{1,0:T(8,128)S(1)}, f32[256,256]{1,0:T(8,128)S(1)}, u32[]{:S(2)}, u32[]{:S(2)}) collective-permute-start(f32[256,256]{1,0:T(8,128)S(1)} %get-tuple-element.121), channel_id=1, source_target_pairs={{0,1},{1,0},{2,3},{3,2},{4,5},{5,4},{6,7},{7,6},{8,9},{9,8},{10,11... | collective-permute-start | bytes 786440 | tf_op jit(solution)/shard_map/ppermute | solution.py:295
  297.7 12.2 %collective-permute-start.14 = (f32[128,256]{1,0:T(8,128)S(1)}, f32[128,256]{1,0:T(8,128)S(1)}, u32[]{:S(2)}, u32[]{:S(2)}) collective-permute-start(f32[128,256]{1,0:T(8,128)S(1)} %dynamic-slice_add_fusion.20), channel_id=1, source_target_pairs={{0,16},{8,24},{16,0},{24,8},{1,17},{9,25},{17,1},{25,9},{2,18},{10... | collective-permute-start | bytes 393224 | tf_op jit(solution)/shard_map/ppermute | solution.py:295
  300.2 12.5 %collective-permute-start.15 = (f32[128,256]{1,0:T(8,128)S(1)}, f32[128,256]{1,0:T(8,128)S(1)}, u32[]{:S(2)}, u32[]{:S(2)}) collective-permute-start(f32[128,256]{1,0:T(8,128)S(1)} %dynamic-slice_add_fusion.19), channel_id=1, source_target_pairs={{0,16},{8,24},{16,0},{24,8},{1,17},{9,25},{17,1},{25,9},{2,18},{10... | collective-permute-start | bytes 393224 | tf_op jit(solution)/shard_map/ppermute | solution.py:295
  300.6 13.9 %collective-permute-start.16 = (f32[128,256]{1,0:T(8,128)S(1)}, f32[128,256]{1,0:T(8,128)S(1)}, u32[]{:S(2)}, u32[]{:S(2)}) collective-permute-start(f32[128,256]{1,0:T(8,128)S(1)} %dynamic-slice_add_fusion.18), channel_id=1, source_target_pairs={{0,16},{8,24},{16,0},{24,8},{1,17},{9,25},{17,1},{25,9},{2,18},{10... | collective-permute-start | bytes 393224 | tf_op jit(solution)/shard_map/ppermute | solution.py:295
  314.7 13.8 %collective-permute-start.17 = (f32[128,256]{1,0:T(8,128)S(1)}, f32[128,256]{1,0:T(8,128)S(1)}, u32[]{:S(2)}, u32[]{:S(2)}) collective-permute-start(f32[128,256]{1,0:T(8,128)S(1)} %add_add_fusion.2), channel_id=1, source_target_pairs={{0,16},{8,24},{16,0},{24,8},{1,17},{9,25},{17,1},{25,9},{2,18},{10... | collective-permute-start | bytes 393224 | tf_op jit(solution)/shard_map/ppermute | solution.py:295
  314.8 16.5 %collective-permute-start.18 = (f32[128,256]{1,0:T(8,128)S(1)}, f32[128,256]{1,0:T(8,128)S(1)}, u32[]{:S(2)}, u32[]{:S(2)}) collective-permute-start(f32[128,256]{1,0:T(8,128)S(1)} %add_add_fusion.1), channel_id=1, source_target_pairs={{0,16},{8,24},{16,0},{24,8},{1,17},{9,25},{17,1},{25,9},{2,18},{10... | collective-permute-start | bytes 393224 | tf_op jit(solution)/shard_map/ppermute | solution.py:295
  317.8 16.3 %collective-permute-start.19 = (f32[128,256]{1,0:T(8,128)S(1)}, f32[128,256]{1,0:T(8,128)S(1)}, u32[]{:S(2)}, u32[]{:S(2)}) collective-permute-start(f32[128,256]{1,0:T(8,128)S(1)} %add_add_fusion), channel_id=1, source_target_pairs={{0,16},{8,24},{16,0},{24,8},{1,17},{9,25},{17,1},{25,9},{2,18},{10... | collective-permute-start | bytes 393224 | tf_op jit(solution)/shard_map/ppermute | solution.py:295
  334.1 8.3 %collective-permute-start.20 = (f32[256,256]{1,0:T(8,128)S(1)}, f32[256,256]{1,0:T(8,128)S(1)}, u32[]{:S(2)}, u32[]{:S(2)}) collective-permute-start(f32[256,256]{1,0:T(8,128)S(1)} %constant_dynamic-update-slice_fusion.4), channel_id=1, source_target_pairs={{0,8},{8,0},{16,24},{24,16},{1,9},{9,1},{17,25},{25,17},{2,10},{10... | collective-permute-start | bytes 786440 | tf_op jit(solution)/shard_map/ppermute | solution.py:295
  334.2 8.3 %collective-permute-start.21 = (f32[256,256]{1,0:T(8,128)S(1)}, f32[256,256]{1,0:T(8,128)S(1)}, u32[]{:S(2)}, u32[]{:S(2)}) collective-permute-start(f32[256,256]{1,0:T(8,128)S(1)} %constant_dynamic-update-slice_fusion.2), channel_id=1, source_target_pairs={{0,4},{2,6},{4,0},{6,2},{1,5},{3,7},{5,1},{7,3},{8,12},{10,14},{12... | collective-permute-start | bytes 786440 | tf_op jit(solution)/shard_map/ppermute | solution.py:295
  335.8 7.9 %collective-permute-start.22 = (f32[256,256]{1,0:T(8,128)S(1)}, f32[256,256]{1,0:T(8,128)S(1)}, u32[]{:S(2)}, u32[]{:S(2)}) collective-permute-start(f32[256,256]{1,0:T(8,128)S(1)} %constant_dynamic-update-slice_fusion), channel_id=1, source_target_pairs={{0,1},{1,0},{2,3},{3,2},{4,5},{5,4},{6,7},{7,6},{8,9},{9,8},{10,11... | collective-permute-start | bytes 786440 | tf_op jit(solution)/shard_map/ppermute | solution.py:295
  343.9 12.8 %collective-permute-start.23 = (f32[512,256]{1,0:T(8,128)S(1)}, f32[512,256]{1,0:T(8,128)S(1)}, u32[]{:S(2)}, u32[]{:S(2)}) collective-permute-start(f32[512,256]{1,0:T(8,128)S(1)} %pad_maximum_fusion.3), channel_id=1, source_target_pairs={{0,1},{1,0},{2,3},{3,2},{4,5},{5,4},{6,7},{7,6},{8,9},{9,8},{10,11... | collective-permute-start | bytes 1572872 | tf_op jit(solution)/shard_map/ppermute | solution.py:295
  345.6 12.4 %collective-permute-start.24 = (f32[512,256]{1,0:T(8,128)S(1)}, f32[512,256]{1,0:T(8,128)S(1)}, u32[]{:S(2)}, u32[]{:S(2)}) collective-permute-start(f32[512,256]{1,0:T(8,128)S(1)} %pad_maximum_fusion.4), channel_id=1, source_target_pairs={{0,8},{8,0},{16,24},{24,16},{1,9},{9,1},{17,25},{25,17},{2,10},{10... | collective-permute-start | bytes 1572872 | tf_op jit(solution)/shard_map/ppermute | solution.py:295
  347.2 11.9 %collective-permute-start.25 = (f32[512,256]{1,0:T(8,128)S(1)}, f32[512,256]{1,0:T(8,128)S(1)}, u32[]{:S(2)}, u32[]{:S(2)}) collective-permute-start(f32[512,256]{1,0:T(8,128)S(1)} %pad_maximum_fusion.5), channel_id=1, source_target_pairs={{0,4},{2,6},{4,0},{6,2},{1,5},{3,7},{5,1},{7,3},{8,12},{10,14},{12... | collective-permute-start | bytes 1572872 | tf_op jit(solution)/shard_map/ppermute | solution.py:295
  359.3 22.3 %collective-permute-start.26 = (f32[1024,256]{1,0:T(8,128)S(1)}, f32[1024,256]{1,0:T(8,128)S(1)}, u32[]{:S(2)}, u32[]{:S(2)}) collective-permute-start(f32[1024,256]{1,0:T(8,128)S(1)} %pad_maximum_fusion), channel_id=1, source_target_pairs={{0,4},{2,6},{4,0},{6,2},{1,5},{3,7},{5,1},{7,3},{8,12},{10,14},{12... | collective-permute-start | bytes 3145736 | tf_op jit(solution)/shard_map/ppermute | solution.py:295
  360.0 22.0 %collective-permute-start.27 = (f32[1024,256]{1,0:T(8,128)S(1)}, f32[1024,256]{1,0:T(8,128)S(1)}, u32[]{:S(2)}, u32[]{:S(2)}) collective-permute-start(f32[1024,256]{1,0:T(8,128)S(1)} %pad_maximum_fusion.1), channel_id=1, source_target_pairs={{0,1},{1,0},{2,3},{3,2},{4,5},{5,4},{6,7},{7,6},{8,9},{9,8},{10,11... | collective-permute-start | bytes 3145736 | tf_op jit(solution)/shard_map/ppermute | solution.py:295
  360.4 21.8 %collective-permute-start.28 = (f32[1024,256]{1,0:T(8,128)S(1)}, f32[1024,256]{1,0:T(8,128)S(1)}, u32[]{:S(2)}, u32[]{:S(2)}) collective-permute-start(f32[1024,256]{1,0:T(8,128)S(1)} %pad_maximum_fusion.2), channel_id=1, source_target_pairs={{0,8},{8,0},{16,24},{24,16},{1,9},{9,1},{17,25},{25,17},{2,10},{10... | collective-permute-start | bytes 3145736 | tf_op jit(solution)/shard_map/ppermute | solution.py:295
  364.2 19.8 %collective-permute-start.29 = (f32[3072,256]{1,0:T(8,128)}, f32[3072,256]{1,0:T(8,128)}, u32[]{:S(2)}, u32[]{:S(2)}) collective-permute-start(f32[3072,256]{1,0:T(8,128)} %constant_dynamic-update-slice_fusion.6), channel_id=1, source_target_pairs={{0,2},{2,0},{4,6},{6,4},{1,3},{3,1},{5,7},{7,5},{8,10},{10,8},{12,... | collective-permute-start | bytes 9437192 | tf_op jit(solution)/shard_map/ppermute | solution.py:295
  382.2 5.9 copy-start
  382.2 5.9 collective-permute-start.30
  414.4 23.8 %copy-start.5 = (f32[288,1280]{1,0:T(8,128)S(1)}, f32[288,1280]{1,0:T(8,128)}, u32[]{:S(2)}) copy-start(f32[288,1280]{1,0:T(8,128)} %eager.5) | copy-start | bytes 4423684
  430.0 144.7 %collective-permute-start.35 = (f32[432,1280]{1,0:T(8,128)}, f32[432,1280]{1,0:T(8,128)}, u32[]{:S(2)}, u32[]{:S(2)}) collective-permute-start(f32[432,1280]{1,0:T(8,128)} %eager.6), channel_id=1, source_target_pairs={{0,8},{8,0},{16,24},{24,16},{1,9},{9,1},{17,25},{25,17},{2,10},{10... | collective-permute-start | bytes 6635528 | tf_op jit(solution)/shard_map/ppermute | solution.py:295
  433.4 64.6 %collective-permute-start.32 = (f32[144,1280]{1,0:T(8,128)}, f32[144,1280]{1,0:T(8,128)S(1)}, u32[]{:S(2)}, u32[]{:S(2)}) collective-permute-start(f32[144,1280]{1,0:T(8,128)} %constant_dynamic-slice_fusion.1), channel_id=1, source_target_pairs={{0,16},{8,24},{16,0},{24,8},{1,17},{9,25},{17,1},{25,9},{2,18},{10... | collective-permute-start | bytes 2211848 | tf_op jit(solution)/shard_map/ppermute | solution.py:295
  434.4 81.8 %collective-permute-start.33 = (f32[144,1280]{1,0:T(8,128)}, f32[144,1280]{1,0:T(8,128)S(1)}, u32[]{:S(2)}, u32[]{:S(2)}) collective-permute-start(f32[144,1280]{1,0:T(8,128)} %constant_dynamic-slice_fusion), channel_id=1, source_target_pairs={{0,24},{8,16},{16,8},{24,0},{1,25},{9,17},{17,9},{25,1},{2,26},{10... | collective-permute-start | bytes 2211848 | tf_op jit(solution)/shard_map/ppermute | solution.py:295
  435.9 135.8 %collective-permute-start.36 = (f32[288,1280]{1,0:T(8,128)}, f32[288,1280]{1,0:T(8,128)}, u32[]{:S(2)}, u32[]{:S(2)}) collective-permute-start(f32[288,1280]{1,0:T(8,128)} %eager.4), channel_id=1, source_target_pairs={{0,24},{8,16},{16,8},{24,0},{1,25},{9,17},{17,9},{25,1},{2,26},{10... | collective-permute-start | bytes 4423688 | tf_op jit(solution)/shard_map/ppermute | solution.py:295
  438.2 188.6 %collective-permute-start.31 = (f32[288,1280]{1,0:T(8,128)S(1)}, f32[288,1280]{1,0:T(8,128)}, u32[]{:S(2)}, u32[]{:S(2)}) collective-permute-start(f32[288,1280]{1,0:T(8,128)S(1)} %copy-done.5), channel_id=1, source_target_pairs={{0,16},{8,24},{16,0},{24,8},{1,17},{9,25},{17,1},{25,9},{2,18},{10... | collective-permute-start | bytes 4423688 | tf_op jit(solution)/shard_map/ppermute | solution.py:295
  498.1 18.2 %copy-start.2 = (f32[144,1280]{1,0:T(8,128)}, f32[144,1280]{1,0:T(8,128)S(1)}, u32[]{:S(2)}) copy-start(f32[144,1280]{1,0:T(8,128)S(1)} %collective-permute-done.32.refs_6_) | copy-start | bytes 2211844
  516.2 0.9 copy-start.3
  530.5 61.6 %collective-permute-start.34 = (f32[144,1280]{1,0:T(8,128)}, f32[144,1280]{1,0:T(8,128)S(1)}, u32[]{:S(2)}, u32[]{:S(2)}) collective-permute-start(f32[144,1280]{1,0:T(8,128)} %correction.2), channel_id=1, source_target_pairs={{0,8},{8,0},{16,24},{24,16},{1,9},{9,1},{17,25},{25,17},{2,10},{10... | collective-permute-start | bytes 2211848 | tf_op jit(solution)/shard_map/ppermute | solution.py:295
  592.2 0.9 copy-start.6
